TPU v7x, 32 devices: a whole 2x2x4 slice. The times are simulated.
32 devices in a mesh: groups: 2 (over y), patch: 4 (over z), sub: 4 (over x, core).
Axes of the slice: x: 2, y: 2, z: 4, core: 2. Of those that a mesh axis runs over, the one named last changes fastest.
Arguments:
- fine_nodes: float32 [32768, 128], P(('groups', 'patch', 'sub')), parts along dimension 0, may hold values from -6 to 6
- fine_edges: float32 [32768, 6, 128], P(('groups', 'patch', 'sub')), parts along dimension 0, may hold values from -6 to 6
- fine_senders: int32 [32768, 6], P(('groups', 'patch', 'sub')), parts along dimension 0, may hold values from 0 to 1279
- fine_halo: int32 [64, 128], P(('groups', 'patch', 'sub')), parts along dimension 0, may hold values from 0 to 1023
- fine_pool: int32 [32768], P(('groups', 'patch', 'sub')), parts along dimension 0, may hold values from 0 to 1023, as said below
- quarter_edges: float32 [8192, 4, 128], P(('groups', 'patch')), parts along dimension 0, may hold values from -6 to 6
- quarter_senders: int32 [8192, 4], P(('groups', 'patch')), parts along dimension 0, may hold values from 0 to 1279
- quarter_halo: int32 [16, 128], P(('groups', 'patch')), parts along dimension 0, may hold values from 0 to 1023
- quarter_pool: int32 [8192], P(('groups', 'patch')), parts along dimension 0, may hold values from 0 to 255, as said below
- coarse_edges: float32 [2048, 4, 128], P(('groups', 'patch', 'sub')), parts along dimension 0, may hold values from -6 to 6
- coarse_senders: int32 [2048, 4], P('groups'), parts along dimension 0, may hold values from 0 to 1023
- edge_in: float32 [3, 384, 128], replicated, may hold values from -0.3125 to 0.3125
- edge_out: float32 [3, 128, 128], replicated, may hold values from -0.5 to 0.5
- node_in: float32 [3, 256, 128], replicated, may hold values from -0.375 to 0.375
- node_out: float32 [3, 128, 128], replicated, may hold values from -0.5 to 0.5
Outputs:
- fine_out: float32 [32768, 128], P(('groups', 'patch', 'sub')), parts along dimension 0
There are 2 independent parts, one for each index of `groups`. A program takes and returns all parts, laid end to end along the dimension named above; an argument that names none is the same for every part. Nothing has to cross between parts.
Inputs may be any that keep to these rules, and one draw needn't show every extreme that they name: `fine_pool`: every one of a patch's 1024 quarter nodes is the target of at least one fine node of that patch. `quarter_pool`: every one of a patch's 256 sixteenth nodes is the target of at least one quarter node of that patch.
All inputs are finite; a program needn't handle non-finite values.
Results may differ from a plain program's by a relative error of at most 0.00005.
Values sent between devices are 32-bit elements; how exact they have to be, the bound alone decides.
No kernel may reach another device: no remote copies, remote signals or barrier semaphores. Data moves between devices by JAX's collectives and lax.ppermute only.
A program may use at most 128 MiB of HBM per device.

v0:
```python
import functools

import jax
import jax.numpy as jnp
from jax import lax
from jax.experimental import pallas as pl
from jax.experimental.pallas import tpu as pltpu
from jax.sharding import PartitionSpec as P


f32 = jnp.float32
half = jnp.bfloat16
LANES = 128
EPS = 1e-05


def side(x):
    high = x.astype(half)
    low = (x - high.astype(f32)).astype(half)
    return jnp.concatenate([high, low], axis=1)


def packed(w):
    row = side(w)
    return jnp.concatenate([row, row], axis=0)


def folded(y):
    w = y.shape[1] // 2
    return y[:, :w] + y[:, w:]


def times(a, b):
    return lax.dot_general(a, b, (((1,), (0,)), ((), ())), preferred_element_type=f32)


def centred_columns(w):
    return w - jnp.mean(w, axis=1, keepdims=True)


def inverse_spread(v):
    return lax.rsqrt(jnp.mean(v * v, axis=1, keepdims=True) + EPS)


def down(row):
    n = row.shape[1]
    parts = []
    for start in range(0, n, LANES):
        wide = jnp.broadcast_to(row[:, start : start + LANES], (LANES, LANES))
        parts.append(jnp.transpose(wide).astype(jnp.int16))
    return parts[0] if len(parts) == 1 else jnp.concatenate(parts, axis=0)


def picks(column, size):
    n = column.shape[0]
    lane = lax.broadcasted_iota(jnp.int32, (n, LANES), 1)
    one, zero = jnp.ones((n, LANES), half), jnp.zeros((n, LANES), half)
    parts = [
        jnp.where(column == (lane + start).astype(jnp.int16), one, zero)
        for start in range(0, size, LANES)
    ]
    return jnp.concatenate(parts, axis=1)


def members(row, size):
    n = row.shape[1]
    line = lax.broadcasted_iota(jnp.int32, (size, n), 0).astype(jnp.int16)
    entry = jnp.broadcast_to(row, (size, n)).astype(jnp.int16)
    return jnp.where(entry == line, jnp.ones((size, n), half), jnp.zeros((size, n), half))


def share_of_each(pools, first, size):
    line = (lax.broadcasted_iota(jnp.int32, (size, LANES), 0) + first).astype(jnp.int16)
    one, zero = jnp.ones((size, LANES), half), jnp.zeros((size, LANES), half)
    total = zero
    for pool in pools:
        for r in range(pool.shape[0]):
            entry = jnp.broadcast_to(pool[r : r + 1, :], (size, LANES)).astype(jnp.int16)
            total = total + jnp.where(entry == line, one, zero)
    return 1.0 / times(total, jnp.ones((LANES, LANES), half))


def first_part(degree, tile, sources, lhs, wide, column, edge, reach, before, extra=None):
    for k in range(degree):
        lhs[k * tile : (k + 1) * tile, :sources] = picks(column(k), sources)
        if edge is not None:
            lhs[k * tile : (k + 1) * tile, sources:] = side(edge(k))
    sums = folded(times(lhs[...], wide[...])).reshape(degree, tile, -1)
    for k in range(degree):
        part = sums[k] + reach
        before[k] = part if extra is None else part + extra[k]


def second_part(degree, tile, hidden, edge_sum, receivers, rhs_message, rhs_node, rhs_out):
    message = folded(times(side(hidden), rhs_message))
    message = (message * inverse_spread(message)).reshape(degree, tile, -1)
    total = edge_sum
    for k in range(degree):
        total = total + message[k]
    node = jnp.concatenate([side(receivers), side(total)], axis=1)
    node_hidden = jnp.maximum(folded(times(node, rhs_node)), 0.0)
    update = folded(times(side(node_hidden), rhs_out))
    return receivers + update * inverse_spread(update)


def pack_second(edge_out, node_in, node_out, weights):
    w = edge_out.shape[1]
    weights[0] = packed(centred_columns(edge_out[...]))
    weights[1] = packed(node_in[0:w])
    weights[2] = packed(node_in[w : 2 * w])
    weights[3] = packed(centred_columns(node_out[...]))


def with_halo(degree, tile, rows, margin, beyond, column, before):
    chosen = [picks(column(k) - jnp.int16(rows), 2 * margin) for k in range(degree)]
    sums = folded(times(jnp.concatenate(chosen, axis=0), beyond[...])).reshape(degree, tile, -1)
    parts = [jnp.maximum(sums[k] + before[k], 0.0) for k in range(degree)]
    return jnp.concatenate(parts, axis=0)


def gather_halo(lists, nodes, to_next, to_previous):
    both = side(nodes[...])
    for i, out in enumerate((to_next, to_previous)):
        out[...] = folded(times(picks(down(lists[i : i + 1, :]), nodes.shape[0]), both))


def start_kernel(lists, nodes, edges, pool, to_next, to_previous, early):
    gather_halo(lists, nodes, to_next, to_previous)
    count = edges.shape[0]
    early[:count, :] = edges[...]
    early[count:, :] = pool[...].astype(f32)


def fine_first_kernel(tile, senders, nodes, edges, edge_in, before, edge_sum, wide, reach_rhs, lhs):
    degree = edges.shape[0]
    rows, w = nodes.shape
    i = pl.program_id(0)

    @pl.when(i == 0)
    def _():
        wide[:rows, :] = side(folded(times(side(nodes[...]), packed(edge_in[0, 0:w]))))
        wide[rows:, :] = packed(edge_in[0, 2 * w : 3 * w])
        reach_rhs[...] = packed(edge_in[0, w : 2 * w])

    receivers = nodes[pl.ds(pl.multiple_of(i * tile, tile), tile), :]
    reach = folded(times(side(receivers), reach_rhs[...]))
    total = edges[0]
    for k in range(1, degree):
        total = total + edges[k]
    edge_sum[...] = total
    first_part(
        degree, tile, rows, lhs, wide, lambda k: down(senders[k : k + 1, :]), lambda k: edges[k], reach, before
    )


def rotated(target, flip, part):
    return jnp.where(target < part, target + flip * part, target - flip * part)


def fine_second_kernel(
    tile, flip, senders, pool, nodes, left, right, before, edge_sum, edge_in, edge_out, node_in, node_out,
    new, keep, send, beyond, weights,
):
    degree = before.shape[0]
    rows, w = nodes.shape
    margin = left.shape[0]
    i = pl.program_id(0)

    @pl.when(i == 0)
    def _():
        sender = packed(edge_in[0, 0:w])
        beyond[:margin, :] = side(folded(times(side(left[...]), sender)))
        beyond[margin:, :] = side(folded(times(side(right[...]), sender)))
        pack_second(edge_out.at[0], node_in.at[0], node_out.at[0], weights)
        keep[...] = jnp.zeros_like(keep)
        send[...] = jnp.zeros_like(send)

    receivers = nodes[pl.ds(pl.multiple_of(i * tile, tile), tile), :]
    hidden = with_halo(degree, tile, rows, margin, beyond, lambda k: down(senders[k : k + 1, :]), before)
    updated = second_part(
        degree, tile, hidden, edge_sum[...], receivers, weights[0],
        jnp.concatenate([weights[1], weights[2]], axis=0), weights[3],
    )
    new[...] = updated
    both = side(updated)
    part = keep.shape[0]
    per = tile // LANES
    target = jnp.concatenate([pool[pl.ds(i * per + j, 1), :] for j in range(per)], axis=1)
    target = rotated(target, flip[0], part)
    keep[...] += folded(times(members(target, part), both))
    send[...] += folded(times(members(target - part, part), both))


def window_kernel(n_sub, place, *refs):
    early, refs = refs[:n_sub], refs[n_sub:]
    (quarter_pool, fine_pool, quarter_edges, edge_in, _, share, coarse_share, chosen, quarter_before,
     quarter_sum, coarse_before, coarse_sum, edges) = refs
    w = edge_in.shape[2]
    piece = early[0].shape[0] - fine_pool.shape[0]
    pools = [block[piece:, :].astype(jnp.int32) for block in early]
    share[...] = share_of_each(pools, 0, share.shape[0])
    coarse_part = coarse_share.shape[0]
    coarse_share[...] = share_of_each([quarter_pool[...]], place[1] * coarse_part, coarse_part)

    degree, rows, _ = quarter_before.shape
    rhs = packed(edge_in[1, 2 * w : 3 * w])
    total = None
    for k in range(degree):
        edge = quarter_edges[pl.ds(k, rows, stride=degree), :]
        total = edge if total is None else total + edge
        quarter_before[k] = folded(times(side(edge), rhs))
    quarter_sum[...] = total

    for j in range(n_sub):
        at = lax.rem(place[0] + j, n_sub)
        edges[pl.ds(pl.multiple_of(at * piece, piece), piece), :] = early[j][:piece, :]
    degree, rows, _ = coarse_before.shape
    rhs = packed(edge_in[2, 2 * w : 3 * w])
    total = None
    for k in range(degree):
        edge = edges[pl.ds(k, rows, stride=degree), :]
        total = edge if total is None else total + edge
        coarse_before[k] = folded(times(side(edge), rhs))
    coarse_sum[...] = total

    parent = [down(quarter_pool[r : r + 1, :]) for r in range(quarter_pool.shape[0])]
    parent = side(jnp.concatenate(parent, axis=0).astype(jnp.int32).astype(f32))
    for r in range(fine_pool.shape[0]):
        rows = slice(r * LANES, (r + 1) * LANES)
        named = folded(times(picks(down(fine_pool[r : r + 1, :]), parent.shape[0]), parent))
        chosen[rows, :] = picks(named.astype(jnp.int32).astype(jnp.int16), chosen.shape[1])


def quarter_nodes_kernel(flip, mine, other, share, lists, nodes, to_next, to_previous):
    part = mine.shape[0]
    first = pl.multiple_of(flip[0] * part, part)
    second = pl.multiple_of((1 - flip[0]) * part, part)
    nodes[pl.ds(first, part), :] = mine[...] * share[pl.ds(first, part), :]
    nodes[pl.ds(second, part), :] = other[...] * share[pl.ds(second, part), :]
    gather_halo(lists, nodes, to_next, to_previous)


def quarter_first_kernel(tile, flip, senders, nodes, extra, edge_in, before, wide, lhs):
    degree, part, w = before.shape
    rows = nodes.shape[0]
    wide[...] = side(folded(times(side(nodes[...]), packed(edge_in[1, 0:w]))))
    reach_rhs = packed(edge_in[1, w : 2 * w])
    for t in range(part // tile):
        span = slice(t * tile, (t + 1) * tile)
        receivers = nodes[pl.ds(pl.multiple_of(flip[0] * part + t * tile, tile), tile), :]
        reach = folded(times(side(receivers), reach_rhs))
        first_part(
            degree, tile, rows, lhs, wide, lambda k: down(senders[k : k + 1, span]), None, reach,
            before.at[:, span, :], extra.at[:, span, :],
        )


def quarter_second_kernel(
    tile, flip, senders, pool, nodes, left, right, before, edge_sum, edge_in, edge_out, node_in, node_out,
    new, keep, send, beyond, weights,
):
    degree, part, w = before.shape
    rows = nodes.shape[0]
    margin = left.shape[0]
    sender = packed(edge_in[1, 0:w])
    beyond[:margin, :] = side(folded(times(side(left[...]), sender)))
    beyond[margin:, :] = side(folded(times(side(right[...]), sender)))
    pack_second(edge_out.at[1], node_in.at[1], node_out.at[1], weights)
    per = tile // LANES
    coarse_part = keep.shape[0]
    for t in range(part // tile):
        span = slice(t * tile, (t + 1) * tile)
        receivers = nodes[pl.ds(pl.multiple_of(flip[0] * part + t * tile, tile), tile), :]
        hidden = with_halo(
            degree, tile, rows, margin, beyond, lambda k: down(senders[k : k + 1, span]), before.at[:, span, :]
        )
        updated = second_part(
            degree, tile, hidden, edge_sum[span, :], receivers, weights[0],
            jnp.concatenate([weights[1], weights[2]], axis=0), weights[3],
        )
        new[span, :] = updated
        at = flip[0] * (part // LANES) + t * per
        target = jnp.concatenate([pool[pl.ds(at + j, 1), :] for j in range(per)], axis=1)
        target = rotated(target, flip[0], coarse_part)
        both = side(updated)
        kept = folded(times(members(target, coarse_part), both))
        sent = folded(times(members(target - coarse_part, coarse_part), both))
        keep[...] = kept if t == 0 else keep[...] + kept
        send[...] = sent if t == 0 else send[...] + sent


def fine_out_kernel(flip, pool, mine, other, fine_new, out, nodes):
    part = mine.shape[0]
    nodes[pl.ds(pl.multiple_of(flip[0] * part, part), part), :] = mine[...]
    nodes[pl.ds(pl.multiple_of((1 - flip[0]) * part, part), part), :] = other[...]
    both = side(nodes[...])
    for r in range(pool.shape[0]):
        rows = slice(r * LANES, (r + 1) * LANES)
        out[rows, :] = fine_new[rows, :] + folded(times(picks(down(pool[r : r + 1, :]), both.shape[0]), both))


def coarse_kernel(n_patch, tile, place, *refs):
    mine, refs = refs[:n_patch], refs[n_patch:]
    other, refs = refs[:n_patch], refs[n_patch:]
    (senders, extra, edge_sum, chosen, base, edge_in, edge_out, node_in, node_out,
     out, nodes, wide, weights, lhs, before, new) = refs
    part, w = mine[0].shape
    block = 2 * part
    degree = extra.shape[0]
    sources = nodes.shape[0]
    for j in range(n_patch):
        at = lax.rem(place[0] + j, n_patch) * block
        nodes[pl.ds(pl.multiple_of(at + place[1] * part, part), part), :] = mine[j][...]
        nodes[pl.ds(pl.multiple_of(at + (1 - place[1]) * part, part), part), :] = other[j][...]
    wide[...] = side(folded(times(side(nodes[...]), packed(edge_in[2, 0:w]))))
    reach_rhs = packed(edge_in[2, w : 2 * w])
    pack_second(edge_out.at[2], node_in.at[2], node_out.at[2], weights)
    for t in range(block // tile):
        span = slice(t * tile, (t + 1) * tile)
        receivers = nodes[pl.ds(pl.multiple_of(place[0] * block + t * tile, tile), tile), :]
        reach = folded(times(side(receivers), reach_rhs))
        first_part(
            degree, tile, sources, lhs, wide, lambda k: down(senders[k : k + 1, span]), None, reach, before,
            extra.at[:, span, :],
        )
        hidden = jnp.maximum(before[...], 0.0).reshape(degree * tile, w)
        new[span, :] = second_part(
            degree, tile, hidden, edge_sum[span, :], receivers, weights[0],
            jnp.concatenate([weights[1], weights[2]], axis=0), weights[3],
        )
    out[...] = base[...] + folded(times(chosen[...], side(new[...])))


def whole(*shape):
    return pl.BlockSpec(shape, lambda *_: (0,) * len(shape))


def shaped(*shape, dtype=f32):
    return jax.ShapeDtypeStruct(shape, dtype)


def run(kernel, grid, scalars, in_specs, operands, outs, out_specs, scratch, mega, flops):
    return pl.pallas_call(
        kernel,
        out_shape=outs,
        grid_spec=pltpu.PrefetchScalarGridSpec(
            num_scalar_prefetch=len(scalars), grid=grid, in_specs=in_specs, out_specs=out_specs,
            scratch_shapes=scratch,
        ),
        compiler_params=pltpu.CompilerParams(vmem_limit_bytes=mega * 1024 * 1024),
        cost_estimate=pl.CostEstimate(flops=flops, bytes_accessed=10**6, transcendentals=0),
    )(*scalars, *operands)


def passed(value, axis, steps):
    count = lax.axis_size(axis)
    return lax.ppermute(value, axis, [(s, (s + steps) % count) for s in range(count)])


def swapped(value, axis, bit):
    count = lax.axis_size(axis)
    return lax.ppermute(value, axis, [(s, s ^ bit) for s in range(count)])


def on_device(
    fine_nodes, fine_edges, fine_senders, fine_halo, fine_pool, quarter_edges, quarter_senders,
    quarter_halo, quarter_pool, coarse_edges, coarse_senders, edge_in, edge_out, node_in, node_out,
):
    n_sub, n_patch = lax.axis_size("sub"), lax.axis_size("patch")
    sub, patch = lax.axis_index("sub").astype(jnp.int32), lax.axis_index("patch").astype(jnp.int32)
    rows, degree, w = fine_edges.shape
    q_rows, q_degree, _ = quarter_edges.shape
    margin, q_margin = fine_halo.shape[1], quarter_halo.shape[1]
    piece, c_degree, _ = coarse_edges.shape
    total = coarse_senders.shape[0]
    block = total // n_patch
    part, c_part = q_rows // 2, block // 2
    tile = 256
    c_tile = min(block, tile)
    core = sub % 2
    flip = core.reshape(1)
    sub_core = jnp.stack([sub, core])
    patch_core = jnp.stack([patch, core])
    layers = (edge_in, edge_out, node_in, node_out)
    layer_specs = [whole(*x.shape) for x in layers]
    pool_rows = fine_pool.reshape(rows // LANES, LANES)
    quarter_pool_rows = quarter_pool.reshape(q_rows // LANES, LANES)
    fine_senders, quarter_senders, coarse_senders = fine_senders.T, quarter_senders.T, coarse_senders.T
    own_edges = coarse_edges.reshape(piece * c_degree, w)
    early_rows = piece * c_degree + pool_rows.shape[0]
    big = 14 if total <= 2048 else 60

    hbm = lambda x: pltpu.with_memory_space_constraint(x, pltpu.HBM)
    to_next, to_previous, early = run(
        start_kernel, (), (), [whole(2, margin), whole(rows, w), whole(*own_edges.shape), whole(*pool_rows.shape)],
        (hbm(fine_halo), hbm(fine_nodes), hbm(own_edges), hbm(pool_rows)),
        (shaped(margin, w), shaped(margin, w), shaped(early_rows, w)),
        [whole(margin, w), whole(margin, w), whole(early_rows, w)], [], 8, 10**8,
    )
    left = passed(to_next, ("patch", "sub"), 1)
    right = passed(to_previous, ("patch", "sub"), -1)
    all_early = [early] + [passed(early, "sub", -j) for j in range(1, n_sub)]

    before, edge_sum = run(
        functools.partial(fine_first_kernel, tile), (rows // tile,), (),
        [
            pl.BlockSpec((degree, tile), lambda i: (0, i)), whole(rows, w),
            pl.BlockSpec((degree, tile, w), lambda i: (0, i, 0)), whole(*edge_in.shape),
        ],
        (hbm(fine_senders), hbm(fine_nodes), hbm(fine_edges.transpose(1, 0, 2)), hbm(edge_in)),
        (pltpu.HBM((degree, rows, w), f32), pltpu.HBM((rows, w), f32)),
        [pl.BlockSpec((degree, tile, w), lambda i: (0, i, 0)), pl.BlockSpec((tile, w), lambda i: (i, 0))],
        [
            pltpu.VMEM((rows + 2 * w, 2 * w), half), pltpu.VMEM((2 * w, 2 * w), half),
            pltpu.VMEM((degree * tile, rows + 2 * w), half),
        ],
        16, 8 * 10**9,
    )
    fine_new, keep, send = run(
        functools.partial(fine_second_kernel, tile), (rows // tile,), (flip,),
        [
            pl.BlockSpec((degree, tile), lambda i, *_: (0, i)), whole(*pool_rows.shape), whole(rows, w),
            whole(margin, w), whole(margin, w), pl.BlockSpec((degree, tile, w), lambda i, *_: (0, i, 0)),
            pl.BlockSpec((tile, w), lambda i, *_: (i, 0)), *layer_specs,
        ],
        (fine_senders, pool_rows, fine_nodes, left, right, hbm(before), hbm(edge_sum), *layers),
        (pltpu.HBM((rows, w), f32), shaped(part, w), shaped(part, w)),
        [pl.BlockSpec((tile, w), lambda i, *_: (i, 0)), whole(part, w), whole(part, w)],
        [pltpu.VMEM((2 * margin, 2 * w), half), pltpu.VMEM((4, 2 * w, 2 * w), half)],
        12, 4 * 10**9,
    )

    mine = keep + swapped(send, "sub", 1)
    after = mine
    bit = 2
    while bit < n_sub:
        mine = mine + swapped(mine, "sub", bit)
        bit *= 2
    share, coarse_share, chosen, quarter_before, quarter_sum, coarse_before, coarse_sum = run(
        functools.partial(window_kernel, n_sub), (1,), (sub_core,),
        [
            *[whole(early_rows, w)] * n_sub, whole(*quarter_pool_rows.shape), whole(*pool_rows.shape),
            pl.BlockSpec((part * q_degree, w), lambda i, place: (place[1], 0)), whole(*edge_in.shape),
            pl.BlockSpec(memory_space=pl.ANY),
        ],
        (*all_early, quarter_pool_rows, pool_rows, quarter_edges.reshape(q_rows * q_degree, w), edge_in, after),
        (
            shaped(q_rows, w), shaped(c_part, w), shaped(rows, block, dtype=half), shaped(q_degree, part, w),
            shaped(part, w), shaped(c_degree, block, w), shaped(block, w),
        ),
        [
            whole(q_rows, w), whole(c_part, w), whole(rows, block), whole(q_degree, part, w), whole(part, w),
            whole(c_degree, block, w), whole(block, w),
        ],
        [pltpu.VMEM((block * c_degree, w), f32)], 12, 10**9,
    )
    other = swapped(mine, "sub", 1)

    quarter_nodes, to_next, to_previous = run(
        quarter_nodes_kernel, (), (flip,),
        [whole(part, w), whole(part, w), whole(q_rows, w), whole(2, q_margin)],
        (mine, other, share, quarter_halo),
        (shaped(q_rows, w), shaped(q_margin, w), shaped(q_margin, w)),
        [whole(q_rows, w), whole(q_margin, w), whole(q_margin, w)], [], 8, 10**8,
    )
    left = passed(to_next, "patch", 1)
    right = passed(to_previous, "patch", -1)
    sender_spec = pl.BlockSpec((q_degree, part), lambda i, flip: (0, flip[0]))
    quarter_first = run(
        functools.partial(quarter_first_kernel, tile), (1,), (flip,),
        [sender_spec, whole(q_rows, w), whole(q_degree, part, w), whole(*edge_in.shape)],
        (quarter_senders, quarter_nodes, quarter_before, edge_in),
        shaped(q_degree, part, w), whole(q_degree, part, w),
        [pltpu.VMEM((q_rows, 2 * w), half), pltpu.VMEM((q_degree * tile, q_rows), half)], 12, 3 * 10**9,
    )
    quarter_mine, keep, send = run(
        functools.partial(quarter_second_kernel, tile), (1,), (flip,),
        [
            sender_spec, whole(*quarter_pool_rows.shape), whole(q_rows, w), whole(q_margin, w), whole(q_margin, w),
            whole(q_degree, part, w), whole(part, w), *layer_specs,
        ],
        (quarter_senders, quarter_pool_rows, quarter_nodes, left, right, quarter_first, quarter_sum, *layers),
        (shaped(part, w), shaped(c_part, w), shaped(c_part, w)),
        [whole(part, w), whole(c_part, w), whole(c_part, w)],
        [pltpu.VMEM((2 * q_margin, 2 * w), half), pltpu.VMEM((4, 2 * w, 2 * w), half)], 12, 2 * 10**9,
    )

    own = (keep + swapped(send, "sub", 1)) * coarse_share
    quarter_other = swapped(quarter_mine, "sub", 1)
    pieces = [own] + [passed(own, "patch", -j) for j in range(1, n_patch)]
    partner = [swapped(value, "sub", 1) for value in pieces]
    base = run(
        fine_out_kernel, (), (flip,), [whole(*pool_rows.shape), whole(part, w), whole(part, w), whole(rows, w)],
        (pool_rows, quarter_mine, quarter_other, hbm(fine_new)), shaped(rows, w), whole(rows, w),
        [pltpu.VMEM((q_rows, w), f32)], 12, 10**9,
    )
    return run(
        functools.partial(coarse_kernel, n_patch, c_tile), (1,), (patch_core,),
        [
            *[whole(c_part, w)] * (2 * n_patch), pl.BlockSpec((c_degree, block), lambda i, place: (0, place[0])),
            whole(c_degree, block, w), whole(block, w), whole(rows, block), whole(rows, w), *layer_specs,
        ],
        (*pieces, *partner, coarse_senders, coarse_before, coarse_sum, chosen, base, *layers),
        shaped(rows, w), whole(rows, w),
        [
            pltpu.VMEM((total, w), f32), pltpu.VMEM((total, 2 * w), half), pltpu.VMEM((4, 2 * w, 2 * w), half),
            pltpu.VMEM((c_degree * c_tile, total), half), pltpu.VMEM((c_degree, c_tile, w), f32),
            pltpu.VMEM((block, w), f32),
        ],
        big, 2 * 10**9,
    )


def solution(mesh):
    split = P(("groups", "patch", "sub"))
    patches = P(("groups", "patch"))
    return jax.shard_map(
        on_device,
        mesh=mesh,
        in_specs=(
            split, split, split, split, split, patches, patches, patches, patches, split, P("groups"),
            P(), P(), P(), P(),
        ),
        out_specs=split,
        check_vma=False,
    )
```

profile of v0, /device:TPU:0, one launch (start us, length us, event | category | flops | bytes accessed | tf_op | source)
XLA Modules:
  0.0 71.5 jit_solution(10163785199121661703)
XLA Ops:
  0.0 1.4 %shard_map.145 = (f32[128,128]{1,0:T(8,128)S(1)}, f32[128,128]{1,0:T(8,128)S(1)}, f32[264,128]{1,0:T(8,128)S(1)}) custom-call(s32[2,128]{1,0:T(2,128)} %lists.2, f32[1024,128]{1,0:T(8,128)} %nodes.5, f32[256,128]{1,0:T(8,128)} %bitcast.23, s32[8,128]{1,0:T(8,128)} %bitcast.11), custom_call_target="tpu_custom_call" | custom-call | flops 100000000 | bytes 1000000 | tf_op jit(solution)/shard_map/pallas_call | solution.py:343
  1.4 0.5 collective-permute-start
  2.0 5.0 %collective-permute-start.1 = (f32[128,128]{1,0:T(8,128)S(1)}, f32[128,128]{1,0:T(8,128)S(1)}, u32[]{:S(2)}, u32[]{:S(2)}) collective-permute-start(f32[128,128]{1,0:T(8,128)S(1)} %get-tuple-element.27), channel_id=1, source_target_pairs={{0,15},{1,0},{2,1},{3,2},{4,3},{5,4},{6,5},{7,6},{8,7},{9,8},{10,9... | collective-permute-start | bytes 196616 | tf_op jit(solution)/shard_map/ppermute | solution.py:357
  7.1 8.2 %shard_map.146 = (f32[6,1024,128]{2,1,0:T(8,128)}, f32[1024,128]{1,0:T(8,128)}) custom-call(s32[6,1024]{1,0:T(8,128)} %bitcast.16, f32[1024,128]{1,0:T(8,128)} %nodes.5, f32[6,1024,128]{2,1,0:T(8,128)} %bitcast.24, f32[3,384,128]{2,1,0:T(8,128)} %refs_13_.1), custom_call_target="tpu_custom_call" | custom-call | flops 8000000000 | bytes 1000000 | tf_op jit(solution)/shard_map/pallas_call | solution.py:343
  15.4 7.7 %shard_map.147 = (f32[1024,128]{1,0:T(8,128)}, f32[512,128]{1,0:T(8,128)S(1)}, f32[512,128]{1,0:T(8,128)S(1)}) custom-call(s32[1]{0:T(128)} %bitcast.1.flip, s32[6,1024]{1,0:T(8,128)S(1)} %bitcast.17, s32[8,128]{1,0:T(8,128)S(1)} %bitcast.12, f32[1024,128]{1,0:T(8,128)S(1)} %copy-done, f32[128,128]{1,0:T(8,128)S(1)} %collective-permute-done.left, ...), custom_call_target="tpu_custom_call" | custom-call | flops 4000000000 | bytes 1000000 | tf_op jit(solution)/shard_map/pallas_call | solution.py:343
  23.1 1.5 %collective-permute-done.2 = f32[512,128]{1,0:T(8,128)S(1)} collective-permute-done((f32[512,128]{1,0:T(8,128)S(1)}, f32[512,128]{1,0:T(8,128)S(1)}, u32[]{:S(2)}, u32[]{:S(2)}) %collective-permute-start.2) | collective-permute-done | bytes 262176 | tf_op jit(solution)/shard_map/ppermute | solution.py:362
  24.7 8.3 %collective-permute-done.3 = f32[512,128]{1,0:T(8,128)S(1)} collective-permute-done((f32[512,128]{1,0:T(8,128)S(1)}, f32[512,128]{1,0:T(8,128)S(1)}, u32[]{:S(2)}, u32[]{:S(2)}) %collective-permute-start.3) | collective-permute-done | bytes 262176 | tf_op jit(solution)/shard_map/ppermute | solution.py:362
  33.6 1.7 %collective-permute-start.6 = (f32[264,128]{1,0:T(8,128)S(1)}, f32[264,128]{1,0:T(8,128)S(1)}, u32[]{:S(2)}, u32[]{:S(2)}) collective-permute-start(f32[264,128]{1,0:T(8,128)S(1)} %get-tuple-element.32.refs_0_), channel_id=1, source_target_pairs={{0,2},{1,3},{2,0},{3,1},{4,6},{5,7},{6,4},{7,5},{8,10},{9,11},{10,... | collective-permute-start | bytes 405512 | tf_op jit(solution)/shard_map/ppermute | solution.py:357
  35.4 2.2 %collective-permute-done.5.refs_1_ = f32[264,128]{1,0:T(8,128)S(1)} collective-permute-done((f32[264,128]{1,0:T(8,128)S(1)}, f32[264,128]{1,0:T(8,128)S(1)}, u32[]{:S(2)}, u32[]{:S(2)}) %collective-permute-start.5) | collective-permute-done | bytes 135200 | tf_op jit(solution)/shard_map/ppermute | solution.py:357
  37.5 4.6 %collective-permute-done.6.refs_2_ = f32[264,128]{1,0:T(8,128)S(1)} collective-permute-done((f32[264,128]{1,0:T(8,128)S(1)}, f32[264,128]{1,0:T(8,128)S(1)}, u32[]{:S(2)}, u32[]{:S(2)}) %collective-permute-start.6) | collective-permute-done | bytes 135200 | tf_op jit(solution)/shard_map/ppermute | solution.py:357
  42.1 2.5 %shard_map.148 = (f32[1024,128]{1,0:T(8,128)S(1)}, f32[128,128]{1,0:T(8,128)S(1)}, bf16[1024,256]{1,0:T(8,128)(2,1)S(1)}, f32[4,512,128]{2,1,0:T(8,128)S(1)}, f3...) custom-call(s32[2]{0:T(128)S(1)} %pad_add_fusion.1.place, ...), custom_call_target="tpu_custom_call" | custom-call | flops 1000000000 | bytes 1000000 | tf_op jit(solution)/shard_map/pallas_call | solution.py:343
  45.3 3.6 %collective-permute-start.9 = (f32[128,128]{1,0:T(8,128)S(1)}, f32[128,128]{1,0:T(8,128)S(1)}, u32[]{:S(2)}, u32[]{:S(2)}) collective-permute-start(f32[128,128]{1,0:T(8,128)S(1)} %get-tuple-element.36), channel_id=1, source_target_pairs={{0,12},{4,0},{8,4},{12,8},{1,13},{5,1},{9,5},{13,9},{2,14},{6,2},{... | collective-permute-start | bytes 196616 | tf_op jit(solution)/shard_map/ppermute | solution.py:357
  49.0 1.5 %shard_map.150.before = f32[4,512,128]{2,1,0:T(8,128)S(1)} custom-call(s32[1]{0:T(128)} %bitcast.1.flip, s32[4,1024]{1,0:T(4,128)S(1)} %bitcast.18, f32[1024,128]{1,0:T(8,128)S(1)} %get-tuple-element.34.nodes, f32[4,512,128]{2,1,0:T(8,128)S(1)} %get-tuple-element.37.extra, f32[3,384,128]{2,1,0:T(8,128)S(1)} %copy-done.4), custom_call_target="tpu_custom_call" | custom-call | flops 3000000000 | bytes 1000000 | tf_op jit(solution)/shard_map/pallas_call | solution.py:343
  50.4 0.9 %collective-permute-done.8.left = f32[128,128]{1,0:T(8,128)S(1)} collective-permute-done((f32[128,128]{1,0:T(8,128)S(1)}, f32[128,128]{1,0:T(8,128)S(1)}, u32[]{:S(2)}, u32[]{:S(2)}) %collective-permute-start.8) | collective-permute-done | bytes 65568 | tf_op jit(solution)/shard_map/ppermute | solution.py:357
  51.3 2.3 %shard_map.151 = (f32[512,128]{1,0:T(8,128)S(1)}, f32[128,128]{1,0:T(8,128)S(1)}, f32[128,128]{1,0:T(8,128)S(1)}) custom-call(s32[1]{0:T(128)} %bitcast.1.flip, s32[4,1024]{1,0:T(4,128)S(1)} %bitcast.19, s32[8,128]{1,0:T(8,128)S(1)} %bitcast.22, f32[1024,128]{1,0:T(8,128)S(1)} %get-tuple-element.34.nodes, f32[128,128]{1,0:T(8,128)S(1)} %collective-permute-done.8.left, ...), custom_call_target="tpu_custom_call" | custom-call | flops 2000000000 | bytes 1000000 | tf_op jit(solution)/shard_map/pallas_call | solution.py:343
  53.7 0.5 collective-permute-start.18
  54.2 0.7 %collective-permute-done.10 = f32[128,128]{1,0:T(8,128)S(1)} collective-permute-done((f32[128,128]{1,0:T(8,128)S(1)}, f32[128,128]{1,0:T(8,128)S(1)}, u32[]{:S(2)}, u32[]{:S(2)}) %collective-permute-start.10) | collective-permute-done | bytes 65568 | tf_op jit(solution)/shard_map/ppermute | solution.py:362
  54.9 3.8 %collective-permute-start.11 = (f32[128,128]{1,0:T(8,128)S(1)}, f32[128,128]{1,0:T(8,128)S(1)}, u32[]{:S(2)}, u32[]{:S(2)}) collective-permute-start(f32[128,128]{1,0:T(8,128)S(1)} %add_multiply_fusion.refs_0_), channel_id=1, source_target_pairs={{0,12},{4,0},{8,4},{12,8},{1,13},{5,1},{9,5},{13,9},{2,14},{6,2},{... | collective-permute-start | bytes 196616 | tf_op jit(solution)/shard_map/ppermute | solution.py:357
  58.7 0.6 collective-permute-start.13
  59.4 1.8 %collective-permute-done.11.refs_1_ = f32[128,128]{1,0:T(8,128)S(1)} collective-permute-done((f32[128,128]{1,0:T(8,128)S(1)}, f32[128,128]{1,0:T(8,128)S(1)}, u32[]{:S(2)}, u32[]{:S(2)}) %collective-permute-start.11) | collective-permute-done | bytes 65568 | tf_op jit(solution)/shard_map/ppermute | solution.py:357
  61.3 4.1 %collective-permute-done.12.refs_2_ = f32[128,128]{1,0:T(8,128)S(1)} collective-permute-done((f32[128,128]{1,0:T(8,128)S(1)}, f32[128,128]{1,0:T(8,128)S(1)}, u32[]{:S(2)}, u32[]{:S(2)}) %collective-permute-start.12) | collective-permute-done | bytes 65568 | tf_op jit(solution)/shard_map/ppermute | solution.py:357
  65.4 0.5 collective-permute-start.17
  65.9 1.8 %shard_map.152.refs_12_ = f32[1024,128]{1,0:T(8,128)S(1)} custom-call(s32[1]{0:T(128)} %bitcast.1.flip, s32[8,128]{1,0:T(8,128)S(1)} %bitcast.14, f32[512,128]{1,0:T(8,128)S(1)} %get-tuple-element.45.mine, f32[512,128]{1,0:T(8,128)S(1)} %collective-permute-done.18.other, f32[1024,128]{1,0:T(8,128)} %get-tuple-element.46.fine_new), custom_call_target="tpu_custom_call" | custom-call | flops 1000000000 | bytes 1000000 | tf_op jit(solution)/shard_map/pallas_call | solution.py:343
  67.7 3.7 %shard_map.153 = f32[1024,128]{1,0:T(8,128)} custom-call(s32[2]{0:T(128)S(1)} %pad_add_fusion.place, f32[128,128]{1,0:T(8,128)S(1)} %add_multiply_fusion.refs_0_, f32[128,128]{1,0:T(8,128)S(1)} %collective-permute-done.11.refs_1_, f32[128,128]{1,0:T(8,128)S(1)} %collective-permute-done.12.refs_2_, f32[128,128]{1,0:T(8,128)S(1)} %collective-permute-done.13.refs_3_, ...), custom_call_target="tpu_custom_call" | custom-call | flops 2000000000 | bytes 1000000 | tf_op jit(solution)/shard_map/pallas_call | solution.py:343
  (52 shorter events, 1.5 us)
Async XLA Ops:
  1.4 13.8 %collective-permute-start = (f32[128,128]{1,0:T(8,128)S(1)}, f32[128,128]{1,0:T(8,128)S(1)}, u32[]{:S(2)}, u32[]{:S(2)}) collective-permute-start(f32[128,128]{1,0:T(8,128)S(1)} %get-tuple-element.26), channel_id=1, source_target_pairs={{0,1},{1,2},{2,3},{3,4},{4,5},{5,6},{6,7},{7,8},{8,9},{9,10},{10,1... | collective-permute-start | bytes 196616 | tf_op jit(solution)/shard_map/ppermute | solution.py:357
  2.0 13.3 %collective-permute-start.1 = (f32[128,128]{1,0:T(8,128)S(1)}, f32[128,128]{1,0:T(8,128)S(1)}, u32[]{:S(2)}, u32[]{:S(2)}) collective-permute-start(f32[128,128]{1,0:T(8,128)S(1)} %get-tuple-element.27), channel_id=1, source_target_pairs={{0,15},{1,0},{2,1},{3,2},{4,3},{5,4},{6,5},{7,6},{8,7},{9,8},{10,9... | collective-permute-start | bytes 196616 | tf_op jit(solution)/shard_map/ppermute | solution.py:357
  15.3 26.8 %copy-start.3 = (f32[1024,4,128]{2,1,0:T(4,128)S(1)}, f32[1024,4,128]{2,1,0:T(4,128)}, u32[]{:S(2)}) copy-start(f32[1024,4,128]{2,1,0:T(4,128)} %param.20) | copy-start | bytes 6291460
  15.4 26.8 %copy-start.11 = (s32[1024]{0:T(1024)S(1)}, s32[1024]{0:T(1024)}, u32[]{:S(2)}) copy-start(s32[1024]{0:T(1024)} %param.23) | copy-start | bytes 12292
  23.1 21.6 %copy-start.2 = (s32[2,128]{1,0:T(2,128)S(1)}, s32[2,128]{1,0:T(2,128)}, u32[]{:S(2)}) copy-start(s32[2,128]{1,0:T(2,128)} %lists.3) | copy-start | bytes 3076
  23.1 1.5 %collective-permute-start.2 = (f32[512,128]{1,0:T(8,128)S(1)}, f32[512,128]{1,0:T(8,128)S(1)}, u32[]{:S(2)}, u32[]{:S(2)}) collective-permute-start(f32[512,128]{1,0:T(8,128)S(1)} %get-tuple-element.31), channel_id=1, source_target_pairs={{0,1},{1,0},{2,3},{3,2},{4,5},{5,4},{6,7},{7,6},{8,9},{9,8},{10,11... | collective-permute-start | bytes 786440 | tf_op jit(solution)/shard_map/ppermute | solution.py:362
  24.6 24.4 %copy-start.9 = (s32[1024,4]{0,1:T(4,128)S(1)}, s32[1024,4]{0,1:T(4,128)}, u32[]{:S(2)}) copy-start(s32[1024,4]{0,1:T(4,128)} %param.21) | copy-start | bytes 49156
  24.6 8.4 %collective-permute-start.3 = (f32[512,128]{1,0:T(8,128)S(1)}, f32[512,128]{1,0:T(8,128)S(1)}, u32[]{:S(2)}, u32[]{:S(2)}) collective-permute-start(f32[512,128]{1,0:T(8,128)S(1)} %add.14.refs_8_), channel_id=1, source_target_pairs={{0,2},{1,3},{2,0},{3,1},{4,6},{5,7},{6,4},{7,5},{8,10},{9,11},{10,... | collective-permute-start | bytes 786440 | tf_op jit(solution)/shard_map/ppermute | solution.py:362
  33.1 11.6 %collective-permute-start.4 = (f32[512,128]{1,0:T(8,128)S(1)}, f32[512,128]{1,0:T(8,128)S(1)}, u32[]{:S(2)}, u32[]{:S(2)}) collective-permute-start(f32[512,128]{1,0:T(8,128)S(1)} %add.15.mine), channel_id=1, source_target_pairs={{0,1},{1,0},{2,3},{3,2},{4,5},{5,4},{6,7},{7,6},{8,9},{9,8},{10,11... | collective-permute-start | bytes 786440 | tf_op jit(solution)/shard_map/ppermute | solution.py:362
  33.2 4.4 %collective-permute-start.5 = (f32[264,128]{1,0:T(8,128)S(1)}, f32[264,128]{1,0:T(8,128)S(1)}, u32[]{:S(2)}, u32[]{:S(2)}) collective-permute-start(f32[264,128]{1,0:T(8,128)S(1)} %get-tuple-element.32.refs_0_), channel_id=1, source_target_pairs={{0,3},{1,0},{2,1},{3,2},{4,7},{5,4},{6,5},{7,6},{8,11},{9,8},{10,9... | collective-permute-start | bytes 405512 | tf_op jit(solution)/shard_map/ppermute | solution.py:357
  33.6 8.6 %collective-permute-start.6 = (f32[264,128]{1,0:T(8,128)S(1)}, f32[264,128]{1,0:T(8,128)S(1)}, u32[]{:S(2)}, u32[]{:S(2)}) collective-permute-start(f32[264,128]{1,0:T(8,128)S(1)} %get-tuple-element.32.refs_0_), channel_id=1, source_target_pairs={{0,2},{1,3},{2,0},{3,1},{4,6},{5,7},{6,4},{7,5},{8,10},{9,11},{10,... | collective-permute-start | bytes 405512 | tf_op jit(solution)/shard_map/ppermute | solution.py:357
  35.3 6.8 %collective-permute-start.7 = (f32[264,128]{1,0:T(8,128)S(1)}, f32[264,128]{1,0:T(8,128)S(1)}, u32[]{:S(2)}, u32[]{:S(2)}) collective-permute-start(f32[264,128]{1,0:T(8,128)S(1)} %get-tuple-element.32.refs_0_), channel_id=1, source_target_pairs={{0,1},{1,2},{2,3},{3,0},{4,5},{5,6},{6,7},{7,4},{8,9},{9,10},{10,1... | collective-permute-start | bytes 405512 | tf_op jit(solution)/shard_map/ppermute | solution.py:357
  45.1 6.2 %collective-permute-start.8 = (f32[128,128]{1,0:T(8,128)S(1)}, f32[128,128]{1,0:T(8,128)S(1)}, u32[]{:S(2)}, u32[]{:S(2)}) collective-permute-start(f32[128,128]{1,0:T(8,128)S(1)} %get-tuple-element.35), channel_id=1, source_target_pairs={{0,4},{4,8},{8,12},{12,0},{1,5},{5,9},{9,13},{13,1},{2,6},{6,10},{... | collective-permute-start | bytes 196616 | tf_op jit(solution)/shard_map/ppermute | solution.py:357
  45.3 6.0 %collective-permute-start.9 = (f32[128,128]{1,0:T(8,128)S(1)}, f32[128,128]{1,0:T(8,128)S(1)}, u32[]{:S(2)}, u32[]{:S(2)}) collective-permute-start(f32[128,128]{1,0:T(8,128)S(1)} %get-tuple-element.36), channel_id=1, source_target_pairs={{0,12},{4,0},{8,4},{12,8},{1,13},{5,1},{9,5},{13,9},{2,14},{6,2},{... | collective-permute-start | bytes 196616 | tf_op jit(solution)/shard_map/ppermute | solution.py:357
  53.6 14.1 %copy-start.10 = (s32[1024,4]{0,1:T(4,128)S(1)}, s32[1024,4]{0,1:T(4,128)}, u32[]{:S(2)}) copy-start(s32[1024,4]{0,1:T(4,128)} %param.25) | copy-start | bytes 49156
  53.6 1.3 %collective-permute-start.10 = (f32[128,128]{1,0:T(8,128)S(1)}, f32[128,128]{1,0:T(8,128)S(1)}, u32[]{:S(2)}, u32[]{:S(2)}) collective-permute-start(f32[128,128]{1,0:T(8,128)S(1)} %get-tuple-element.40), channel_id=1, source_target_pairs={{0,1},{1,0},{2,3},{3,2},{4,5},{5,4},{6,7},{7,6},{8,9},{9,8},{10,11... | collective-permute-start | bytes 196616 | tf_op jit(solution)/shard_map/ppermute | solution.py:362
  53.7 12.2 %collective-permute-start.18 = (f32[512,128]{1,0:T(8,128)S(1)}, f32[512,128]{1,0:T(8,128)S(1)}, u32[]{:S(2)}, u32[]{:S(2)}) collective-permute-start(f32[512,128]{1,0:T(8,128)S(1)} %get-tuple-element.45.mine), channel_id=1, source_target_pairs={{0,1},{1,0},{2,3},{3,2},{4,5},{5,4},{6,7},{7,6},{8,9},{9,8},{10,11... | collective-permute-start | bytes 786440 | tf_op jit(solution)/shard_map/ppermute | solution.py:362
  54.9 6.3 %collective-permute-start.11 = (f32[128,128]{1,0:T(8,128)S(1)}, f32[128,128]{1,0:T(8,128)S(1)}, u32[]{:S(2)}, u32[]{:S(2)}) collective-permute-start(f32[128,128]{1,0:T(8,128)S(1)} %add_multiply_fusion.refs_0_), channel_id=1, source_target_pairs={{0,12},{4,0},{8,4},{12,8},{1,13},{5,1},{9,5},{13,9},{2,14},{6,2},{... | collective-permute-start | bytes 196616 | tf_op jit(solution)/shard_map/ppermute | solution.py:357
  58.7 6.6 %collective-permute-start.12 = (f32[128,128]{1,0:T(8,128)S(1)}, f32[128,128]{1,0:T(8,128)S(1)}, u32[]{:S(2)}, u32[]{:S(2)}) collective-permute-start(f32[128,128]{1,0:T(8,128)S(1)} %add_multiply_fusion.refs_0_), channel_id=1, source_target_pairs={{0,8},{4,12},{8,0},{12,4},{1,9},{5,13},{9,1},{13,5},{2,10},{6,14},... | collective-permute-start | bytes 196616 | tf_op jit(solution)/shard_map/ppermute | solution.py:357
  58.7 6.6 %collective-permute-start.13 = (f32[128,128]{1,0:T(8,128)S(1)}, f32[128,128]{1,0:T(8,128)S(1)}, u32[]{:S(2)}, u32[]{:S(2)}) collective-permute-start(f32[128,128]{1,0:T(8,128)S(1)} %add_multiply_fusion.refs_0_), channel_id=1, source_target_pairs={{0,4},{4,8},{8,12},{12,0},{1,5},{5,9},{9,13},{13,1},{2,6},{6,10},{... | collective-permute-start | bytes 196616 | tf_op jit(solution)/shard_map/ppermute | solution.py:357
  59.4 8.2 %collective-permute-start.14 = (f32[128,128]{1,0:T(8,128)S(1)}, f32[128,128]{1,0:T(8,128)S(1)}, u32[]{:S(2)}, u32[]{:S(2)}) collective-permute-start(f32[128,128]{1,0:T(8,128)S(1)} %add_multiply_fusion.refs_0_), channel_id=1, source_target_pairs={{0,1},{1,0},{2,3},{3,2},{4,5},{5,4},{6,7},{7,6},{8,9},{9,8},{10,11... | collective-permute-start | bytes 196616 | tf_op jit(solution)/shard_map/ppermute | solution.py:362
  61.3 6.4 %collective-permute-start.15 = (f32[128,128]{1,0:T(8,128)S(1)}, f32[128,128]{1,0:T(8,128)S(1)}, u32[]{:S(2)}, u32[]{:S(2)}) collective-permute-start(f32[128,128]{1,0:T(8,128)S(1)} %collective-permute-done.11.refs_1_), channel_id=1, source_target_pairs={{0,1},{1,0},{2,3},{3,2},{4,5},{5,4},{6,7},{7,6},{8,9},{9,8},{10,11... | collective-permute-start | bytes 196616 | tf_op jit(solution)/shard_map/ppermute | solution.py:362
  65.3 2.4 %collective-permute-start.16 = (f32[128,128]{1,0:T(8,128)S(1)}, f32[128,128]{1,0:T(8,128)S(1)}, u32[]{:S(2)}, u32[]{:S(2)}) collective-permute-start(f32[128,128]{1,0:T(8,128)S(1)} %collective-permute-done.12.refs_2_), channel_id=1, source_target_pairs={{0,1},{1,0},{2,3},{3,2},{4,5},{5,4},{6,7},{7,6},{8,9},{9,8},{10,11... | collective-permute-start | bytes 196616 | tf_op jit(solution)/shard_map/ppermute | solution.py:362
  65.4 2.4 %collective-permute-start.17 = (f32[128,128]{1,0:T(8,128)S(1)}, f32[128,128]{1,0:T(8,128)S(1)}, u32[]{:S(2)}, u32[]{:S(2)}) collective-permute-start(f32[128,128]{1,0:T(8,128)S(1)} %collective-permute-done.13.refs_3_), channel_id=1, source_target_pairs={{0,1},{1,0},{2,3},{3,2},{4,5},{5,4},{6,7},{7,6},{8,9},{9,8},{10,11... | collective-permute-start | bytes 196616 | tf_op jit(solution)/shard_map/ppermute | solution.py:362
  (7 other events, 58.0 us)
where the time goes:
time: 71.7 us; the launch traced here: 71.5 us
  Pallas kernels  29.6 us (41%)
  waiting for transfers between devices  24.1 us (34%)
  starting transfers between devices  17.2 us (24%)
    pallas_call x9, Pallas kernels, run(): pl.pallas_call(kernel, out_shape=outs, grid_spec=pltpu.PrefetchScalarGrid...  29.6 us
    ppermute x10, starting transfers between devices, passed(): lax.ppermute(value, axis, [(s, (s + steps) % count) for s in range(count)])  16 us
    ppermute x10, waiting for transfers between devices, passed(): lax.ppermute(value, axis, [(s, (s + steps) % count) for s in range(count)])  13.5 us
    ppermute x9, waiting for transfers between devices, swapped(): return lax.ppermute(value, axis, [(s, s ^ bit) for s in range(count)])  10.6 us
  transfers between devices with their start and end apart: 19, of which 8 were waited for; matrix products, arithmetic and copies ran while one was open for 0% of the time, Pallas kernels for 20%

commit v1 on v0

v1 whole, which is shorter than its diff:
```python
import functools

import jax
import jax.numpy as jnp
from jax import lax
from jax.experimental import pallas as pl
from jax.experimental.pallas import tpu as pltpu
from jax.sharding import PartitionSpec as P


f32 = jnp.float32
half = jnp.bfloat16
LANES = 128
EPS = 1e-05


def side(x):
    high = x.astype(half)
    low = (x - high.astype(f32)).astype(half)
    return jnp.concatenate([high, low], axis=1)


def packed(w):
    row = side(w)
    return jnp.concatenate([row, row], axis=0)


def folded(y):
    w = y.shape[1] // 2
    return y[:, :w] + y[:, w:]


def times(a, b):
    return lax.dot_general(a, b, (((1,), (0,)), ((), ())), preferred_element_type=f32)


def centred_columns(w):
    return w - jnp.mean(w, axis=1, keepdims=True)


def inverse_spread(v):
    return lax.rsqrt(jnp.mean(v * v, axis=1, keepdims=True) + EPS)


def down(row):
    n = row.shape[1]
    parts = []
    for start in range(0, n, LANES):
        wide = jnp.broadcast_to(row[:, start : start + LANES], (LANES, LANES))
        parts.append(jnp.transpose(wide).astype(jnp.int16))
    return parts[0] if len(parts) == 1 else jnp.concatenate(parts, axis=0)


def picks(column, size):
    n = column.shape[0]
    lane = lax.broadcasted_iota(jnp.int32, (n, LANES), 1)
    one, zero = jnp.ones((n, LANES), half), jnp.zeros((n, LANES), half)
    parts = [
        jnp.where(column == (lane + start).astype(jnp.int16), one, zero)
        for start in range(0, size, LANES)
    ]
    return jnp.concatenate(parts, axis=1)


def members(row, size):
    n = row.shape[1]
    line = lax.broadcasted_iota(jnp.int32, (size, n), 0).astype(jnp.int16)
    entry = jnp.broadcast_to(row, (size, n)).astype(jnp.int16)
    return jnp.where(entry == line, jnp.ones((size, n), half), jnp.zeros((size, n), half))


def counts_of(pools, first, size):
    line = (lax.broadcasted_iota(jnp.int32, (size, LANES), 0) + first).astype(jnp.int16)
    one, zero = jnp.ones((size, LANES), half), jnp.zeros((size, LANES), half)
    total = zero
    for pool in pools:
        for r in range(pool.shape[0]):
            entry = jnp.broadcast_to(pool[r : r + 1, :], (size, LANES)).astype(jnp.int16)
            total = total + jnp.where(entry == line, one, zero)
    return times(total, jnp.ones((LANES, LANES), half))


def along_lanes(pool, first, lines):
    rows, n = pool.shape
    column = jnp.concatenate([down(pool[r : r + 1, :]) for r in range(rows)], axis=0)
    lane = lax.broadcasted_iota(jnp.int32, (rows * n, LANES), 1) + first
    one, zero = jnp.ones((rows * n, LANES), half), jnp.zeros((rows * n, LANES), half)
    out = []
    for r in range(lines):
        hits = jnp.where(column == (lane + r * LANES).astype(jnp.int16), one, zero)
        out.append(times(jnp.ones((8, rows * n), half), hits)[0:1, :])
    return jnp.concatenate(out, axis=0)


def first_part(degree, tile, lhs, wide, column, reach, before, extra):
    sources = wide.shape[0]
    for k in range(degree):
        lhs[k * tile : (k + 1) * tile, :] = picks(column(k), sources)
    sums = folded(times(lhs[...], wide[...])).reshape(degree, tile, -1)
    for k in range(degree):
        before[k][...] = sums[k] + reach + extra[k]


def second_part(degree, tile, hidden, edge_sum, receivers, weights):
    message = folded(times(side(hidden), weights[0]))
    message = (message * inverse_spread(message)).reshape(degree, tile, -1)
    total = edge_sum
    for k in range(degree):
        total = total + message[k]
    node = jnp.concatenate([side(receivers), side(total)], axis=1)
    rhs_node = jnp.concatenate([weights[1], weights[2]], axis=0)
    node_hidden = jnp.maximum(folded(times(node, rhs_node)), 0.0)
    update = folded(times(side(node_hidden), weights[3]))
    return receivers + update * inverse_spread(update)


def pack_first(edge_in, weights):
    w = edge_in.shape[1]
    weights[0] = packed(edge_in[0:w])
    weights[1] = packed(edge_in[w : 2 * w])


def pack_second(edge_out, node_in, node_out, weights):
    w = edge_out.shape[1]
    weights[0] = packed(centred_columns(edge_out[...]))
    weights[1] = packed(node_in[0:w])
    weights[2] = packed(node_in[w : 2 * w])
    weights[3] = packed(centred_columns(node_out[...]))


def with_halo(degree, tile, rows, margin, beyond, column, before):
    chosen = [picks(column(k) - jnp.int16(rows), 2 * margin) for k in range(degree)]
    sums = folded(times(jnp.concatenate(chosen, axis=0), beyond[...])).reshape(degree, tile, -1)
    parts = [jnp.maximum(sums[k] + before[k][...], 0.0) for k in range(degree)]
    return jnp.concatenate(parts, axis=0)


def halo_sources(left, right, sender, beyond):
    margin = left.shape[0]
    beyond[:margin, :] = side(folded(times(side(left[...]), sender)))
    beyond[margin:, :] = side(folded(times(side(right[...]), sender)))


def rotated(target, flip, part):
    return jnp.where(target < part, target + flip * part, target - flip * part)


def gather_halo(lists, nodes, to_next, to_previous):
    both = side(nodes[...])
    for i, out in enumerate((to_next, to_previous)):
        out[...] = folded(times(picks(down(lists[i : i + 1, :]), nodes.shape[0]), both))


def start_kernel(lists, nodes, senders, pool, edge_in, to_next, to_previous, kept_nodes, kept_senders, kept_pool, weights):
    gather_halo(lists, nodes, to_next, to_previous)
    kept_nodes[...] = nodes[...]
    kept_senders[...] = senders[...]
    kept_pool[...] = pool[...]
    pack_first(edge_in.at[0], weights)
    w = nodes.shape[1]
    weights[2] = packed(edge_in[0, 2 * w : 3 * w])


def fine_first_kernel(lines, flip, senders, nodes, pool, weights, edges, *refs):
    degree = edges.shape[0]
    before, refs = refs[:degree], refs[degree:]
    columns, refs = refs[:degree], refs[degree:]
    edge_sum, counts, wide, lhs, local, arrived = refs
    rows, _ = nodes.shape
    copies = [pltpu.make_async_copy(edges.at[k], local.at[k], arrived.at[k]) for k in range(degree)]
    for copy in copies:
        copy.start()
    wide[:rows, :] = side(folded(times(side(nodes[...]), weights[0])))
    wide[rows:, :] = weights[2]
    reach = folded(times(side(nodes[...]), weights[1]))
    part = lines * LANES
    height = counts.shape[0] // 2
    counts[...] = jnp.zeros_like(counts)
    counts[:lines, :] = along_lanes(pool, flip[0] * part, lines)
    counts[height : height + lines, :] = along_lanes(pool, (1 - flip[0]) * part, lines)
    for k in range(degree):
        columns[k][...] = jnp.concatenate(
            [down(senders[k : k + 1, start : start + LANES]) for start in range(0, rows, LANES)], axis=0
        )
        copies[k].wait()
        lhs[k % 2, :, :rows] = picks(columns[k][...], rows)
        lhs[k % 2, :, rows:] = side(local[k])
        before[k][...] = folded(times(lhs[k % 2], wide[...])) + reach
        edge_sum[...] = local[k] if k == 0 else edge_sum[...] + local[k]


def fine_second_kernel(degree, flip, pool, nodes, left, right, counts, first_weights, *refs):
    before, refs = refs[:degree], refs[degree:]
    columns, refs = refs[:degree], refs[degree:]
    edge_sum, edge_out, node_in, node_out, new, keep, send, beyond, weights, held, sent = refs
    rows, _ = nodes.shape
    margin = left.shape[0]
    halo_sources(left, right, first_weights[0], beyond)
    pack_second(edge_out.at[0], node_in.at[0], node_out.at[0], weights)
    hidden = with_halo(degree, rows, rows, margin, beyond, lambda k: columns[k][...], before)
    held[...] = second_part(degree, rows, hidden, edge_sum[...], nodes[...], weights)
    copy = pltpu.make_async_copy(held, new, sent)
    copy.start()
    both = side(held[...])
    height = counts.shape[0] // 2
    part = keep.shape[0] - height
    target = jnp.concatenate([pool[j : j + 1, :] for j in range(pool.shape[0])], axis=1)
    target = rotated(target, flip[0], part)
    send[:part, :] = folded(times(members(target - part, part), both))
    keep[:part, :] = folded(times(members(target, part), both))
    keep[part:, :] = counts[:height, :]
    send[part:, :] = counts[height:, :]
    copy.wait()


def window_kernel(
    flip, quarter_pool, fine_pool, quarter_edges, quarter_senders, coarse_senders, edge_in, edge_out, node_in, node_out, _,
    coarse_share, chosen, quarter_before, quarter_sum, quarter_columns, coarse_columns, fine_columns,
    quarter_first, quarter_second, coarse_first, coarse_second,
):
    w = edge_in.shape[2]
    block = coarse_share.shape[0]
    share = 1.0 / counts_of([quarter_pool[...]], 0, block)
    coarse_share[...] = share

    degree, rows, _ = quarter_before.shape
    rhs = packed(edge_in[1, 2 * w : 3 * w])
    total = None
    for k in range(degree):
        edge = quarter_edges[pl.ds(k, rows, stride=degree), :]
        total = edge if total is None else total + edge
        quarter_before[k] = folded(times(side(edge), rhs))
    quarter_sum[...] = total
    pack_first(edge_in.at[1], quarter_first)
    pack_second(edge_out.at[1], node_in.at[1], node_out.at[1], quarter_second)
    pack_first(edge_in.at[2], coarse_first)
    coarse_first[2] = packed(edge_in[2, 2 * w : 3 * w])
    pack_second(edge_out.at[2], node_in.at[2], node_out.at[2], coarse_second)

    for k in range(degree):
        for start in range(0, rows, LANES):
            quarter_columns[k, start : start + LANES, :] = down(quarter_senders[k : k + 1, start : start + LANES])
    for k in range(coarse_columns.shape[0]):
        for start in range(0, block, LANES):
            coarse_columns[k, start : start + LANES, :] = down(coarse_senders[k : k + 1, start : start + LANES])

    parent = [down(quarter_pool[r : r + 1, :]) for r in range(quarter_pool.shape[0])]
    parent = side(jnp.concatenate(parent, axis=0).astype(jnp.int32).astype(f32))
    for r in range(fine_pool.shape[0]):
        rows = slice(r * LANES, (r + 1) * LANES)
        column = down(fine_pool[r : r + 1, :])
        fine_columns[rows, :] = column
        named = folded(times(picks(column, parent.shape[0]), parent))
        chosen[rows, :] = picks(named.astype(jnp.int32).astype(jnp.int16), chosen.shape[1])


def mean_kernel(lines, mine, theirs, out):
    part = out.shape[0]
    counts = mine[part : part + lines, :] + theirs[part : part + lines, :]
    for r in range(lines):
        rows = slice(r * LANES, (r + 1) * LANES)
        share = 1.0 / jnp.transpose(jnp.broadcast_to(counts[r : r + 1, :], (LANES, LANES)))
        out[rows, :] = (mine[rows, :] + theirs[rows, :]) * share


def quarter_nodes_kernel(flip, mine, other, lists, nodes, to_next, to_previous):
    part = mine.shape[0]
    nodes[pl.ds(pl.multiple_of(flip[0] * part, part), part), :] = mine[...]
    nodes[pl.ds(pl.multiple_of((1 - flip[0]) * part, part), part), :] = other[...]
    gather_halo(lists, nodes, to_next, to_previous)


def quarter_first_kernel(tile, columns, nodes, mine, extra, weights, before, wide, lhs):
    degree, part, _ = before.shape
    wide[...] = side(folded(times(side(nodes[...]), weights[0])))
    for t in range(part // tile):
        span = slice(t * tile, (t + 1) * tile)
        reach = folded(times(side(mine[span, :]), weights[1]))
        first_part(
            degree, tile, lhs, wide, lambda k: columns[k, span, :], reach,
            [before.at[k, span, :] for k in range(degree)], extra.at[:, span, :],
        )


def quarter_second_kernel(
    flip, columns, pool, mine, left, right, before, edge_sum, first_weights, weights, new, keep, both, beyond,
):
    degree, part, _ = before.shape
    margin = left.shape[0]
    halo_sources(left, right, first_weights[0], beyond)
    hidden = with_halo(
        degree, part, 2 * part, margin, beyond, lambda k: columns[k], [before.at[k] for k in range(degree)]
    )
    updated = second_part(degree, part, hidden, edge_sum[...], mine[...], weights)
    new[...] = updated
    coarse_part = keep.shape[0]
    at = flip[0] * (part // LANES)
    target = jnp.concatenate([pool[pl.ds(at + j, 1), :] for j in range(part // LANES)], axis=1)
    target = rotated(target, flip[0], coarse_part)
    split = side(updated)
    both[:coarse_part, :] = folded(times(members(target - coarse_part, coarse_part), split))
    kept = folded(times(members(target, coarse_part), split))
    both[coarse_part:, :] = kept
    keep[...] = kept


def base_kernel(n_sub, place, columns, mine, other, fine_new, weights, *refs):
    pieces, refs = refs[:n_sub], refs[n_sub:]
    out, before, edge_sum, nodes, edges = refs
    part = mine.shape[0]
    piece = pieces[0].shape[0]
    for j in range(n_sub):
        at = jnp.bitwise_xor(place[0], j)
        edges[pl.ds(pl.multiple_of(at * piece, piece), piece), :] = pieces[j][...]
    degree, block, _ = before.shape
    total = None
    for k in range(degree):
        edge = edges[pl.ds(k, block, stride=degree), :]
        total = edge if total is None else total + edge
        before[k] = folded(times(side(edge), weights[2]))
    edge_sum[...] = total
    nodes[pl.ds(pl.multiple_of(place[1] * part, part), part), :] = mine[...]
    nodes[pl.ds(pl.multiple_of((1 - place[1]) * part, part), part), :] = other[...]
    both = side(nodes[...])
    out[...] = fine_new[...] + folded(times(picks(columns[...], both.shape[0]), both))


def coarse_kernel(n_patch, tile, place, *refs):
    mine, refs = refs[:n_patch], refs[n_patch:]
    other, refs = refs[:n_patch], refs[n_patch:]
    (columns, extra, edge_sum, chosen, base, first_weights, weights,
     out, nodes, wide, lhs, before, new, held, sent) = refs
    part, w = mine[0].shape
    block = 2 * part
    degree = extra.shape[0]
    for j in range(n_patch):
        at = lax.rem(place[0] + j, n_patch) * block
        nodes[pl.ds(pl.multiple_of(at + place[1] * part, part), part), :] = mine[j][...]
        nodes[pl.ds(pl.multiple_of(at + (1 - place[1]) * part, part), part), :] = other[j][...]
    wide[...] = side(folded(times(side(nodes[...]), first_weights[0])))
    for t in range(block // tile):
        span = slice(t * tile, (t + 1) * tile)
        receivers = nodes[pl.ds(pl.multiple_of(place[0] * block + t * tile, tile), tile), :]
        reach = folded(times(side(receivers), first_weights[1]))
        first_part(
            degree, tile, lhs, wide, lambda k: columns[k, span, :], reach,
            [before.at[k] for k in range(degree)], extra.at[:, span, :],
        )
        hidden = jnp.maximum(before[...], 0.0).reshape(degree * tile, w)
        new[span, :] = second_part(degree, tile, hidden, edge_sum[span, :], receivers, weights)
    both = side(new[...])
    steps = sent.shape[0]
    rows = out.shape[0] // steps
    copies = []
    for i in range(steps):
        span = slice(i * rows, (i + 1) * rows)
        held[span, :] = base[span, :] + folded(times(chosen[span, :], both))
        copies.append(pltpu.make_async_copy(held.at[span, :], out.at[span, :], sent.at[i]))
        copies[-1].start()
    for copy in copies:
        copy.wait()


def whole(*shape):
    return pl.BlockSpec(shape, lambda *_: (0,) * len(shape))


def shaped(*shape, dtype=f32):
    return jax.ShapeDtypeStruct(shape, dtype)


def run(kernel, grid, scalars, in_specs, operands, outs, out_specs, scratch, mega, flops):
    return pl.pallas_call(
        kernel,
        out_shape=outs,
        grid_spec=pltpu.PrefetchScalarGridSpec(
            num_scalar_prefetch=len(scalars), grid=grid, in_specs=in_specs, out_specs=out_specs,
            scratch_shapes=scratch,
        ),
        compiler_params=pltpu.CompilerParams(vmem_limit_bytes=mega * 1024 * 1024),
        cost_estimate=pl.CostEstimate(flops=flops, bytes_accessed=10**6, transcendentals=0),
    )(*scalars, *operands)


def passed(value, axis, steps):
    count = lax.axis_size(axis)
    return lax.ppermute(value, axis, [(s, (s + steps) % count) for s in range(count)])


def swapped(value, axis, bit):
    count = lax.axis_size(axis)
    return lax.ppermute(value, axis, [(s, s ^ bit) for s in range(count)])


def on_device(
    fine_nodes, fine_edges, fine_senders, fine_halo, fine_pool, quarter_edges, quarter_senders,
    quarter_halo, quarter_pool, coarse_edges, coarse_senders, edge_in, edge_out, node_in, node_out,
):
    n_sub, n_patch = lax.axis_size("sub"), lax.axis_size("patch")
    sub, patch = lax.axis_index("sub").astype(jnp.int32), lax.axis_index("patch").astype(jnp.int32)
    rows, degree, w = fine_edges.shape
    q_rows, q_degree, _ = quarter_edges.shape
    margin, q_margin = fine_halo.shape[1], quarter_halo.shape[1]
    piece, c_degree, _ = coarse_edges.shape
    total = coarse_senders.shape[0]
    block = total // n_patch
    part, c_part = q_rows // 2, block // 2
    tile = min(256, part)
    c_tile = min(256, block)
    lines = part // LANES
    height = -(-lines // 8) * 8
    core = sub % 2
    flip = core.reshape(1)
    sub_core = jnp.stack([sub, core])
    patch_core = jnp.stack([patch, core])
    layers = (edge_in, edge_out, node_in, node_out)
    layer_specs = [whole(*x.shape) for x in layers]
    in_hbm = pl.BlockSpec(memory_space=pl.ANY)
    pool_rows = fine_pool.reshape(rows // LANES, LANES)
    quarter_pool_rows = quarter_pool.reshape(q_rows // LANES, LANES)
    fine_senders, quarter_senders, coarse_senders = fine_senders.T, quarter_senders.T, coarse_senders.T
    own_edges = coarse_edges.reshape(piece * c_degree, w)
    hbm = lambda x: pltpu.with_memory_space_constraint(x, pltpu.HBM)
    mats = lambda n: (n, 2 * w, 2 * w)
    short = jnp.int16
    big = 16 if total <= 2048 else 48

    to_next, to_previous, nodes, senders, pool, fine_weights = run(
        start_kernel, (1,), (),
        [
            whole(2, margin), whole(rows, w), whole(degree, rows), whole(*pool_rows.shape),
            pl.BlockSpec((1, 3 * w, w), lambda i: (0, 0, 0)),
        ],
        (hbm(fine_halo), hbm(fine_nodes), hbm(fine_senders), hbm(pool_rows), hbm(edge_in)),
        (
            shaped(margin, w), shaped(margin, w), shaped(rows, w), shaped(degree, rows, dtype=jnp.int32),
            shaped(*pool_rows.shape, dtype=jnp.int32), shaped(*mats(3), dtype=half),
        ),
        [
            whole(margin, w), whole(margin, w), whole(rows, w), whole(degree, rows), whole(*pool_rows.shape),
            whole(*mats(3)),
        ],
        [], 8, 10**8,
    )
    left = passed(to_next, ("patch", "sub"), 1)
    right = passed(to_previous, ("patch", "sub"), -1)
    firsts = run(
        functools.partial(fine_first_kernel, lines), (1,), (flip,),
        [whole(degree, rows), whole(rows, w), whole(*pool_rows.shape), whole(*mats(3)), in_hbm],
        (senders, nodes, pool, fine_weights, hbm(fine_edges.transpose(1, 0, 2))),
        (
            *(shaped(rows, w),) * degree, *(shaped(rows, w, dtype=short),) * degree, shaped(rows, w),
            shaped(2 * height, w),
        ),
        [whole(rows, w)] * (2 * degree + 1) + [whole(2 * height, w)],
        [
            pltpu.VMEM((rows + 2 * w, 2 * w), half), pltpu.VMEM((2, rows, rows + 2 * w), half),
            pltpu.VMEM((degree, rows, w), f32), pltpu.SemaphoreType.DMA((degree,)),
        ],
        30, 8 * 10**9,
    )
    before, columns, (edge_sum, counts) = firsts[:degree], firsts[degree : 2 * degree], firsts[2 * degree :]
    fine_new, keep, send = run(
        functools.partial(fine_second_kernel, degree), (1,), (flip,),
        [
            whole(*pool_rows.shape), whole(rows, w), whole(margin, w), whole(margin, w), whole(2 * height, w),
            whole(*mats(3)), *[whole(rows, w)] * (2 * degree + 1), *layer_specs[1:],
        ],
        (pool, nodes, left, right, counts, fine_weights, *before, *columns, edge_sum, *layers[1:]),
        (pltpu.HBM((rows, w), f32), shaped(part + height, w), shaped(part + height, w)),
        [in_hbm, whole(part + height, w), whole(part + height, w)],
        [
            pltpu.VMEM((2 * margin, 2 * w), half), pltpu.VMEM(mats(4), half), pltpu.VMEM((rows, w), f32),
            pltpu.SemaphoreType.DMA,
        ],
        30, 4 * 10**9,
    )

    mine, theirs = keep, swapped(send, "sub", 1)
    bit = 2
    after = theirs
    while bit < n_sub:
        mine = mine + theirs
        theirs = swapped(mine, "sub", bit)
        after = mine if bit == 2 else after
        bit *= 2
    (coarse_share, chosen, quarter_before, quarter_sum, quarter_columns, coarse_columns, fine_columns,
     quarter_weights, quarter_later, coarse_weights, coarse_later) = run(
        window_kernel, (1,), (patch_core,),
        [
            whole(*quarter_pool_rows.shape), whole(*pool_rows.shape),
            pl.BlockSpec((part * q_degree, w), lambda i, place: (place[1], 0)),
            pl.BlockSpec((q_degree, part), lambda i, place: (0, place[1])),
            pl.BlockSpec((c_degree, block), lambda i, place: (0, place[0])), *layer_specs, in_hbm,
        ],
        (quarter_pool_rows, pool, quarter_edges.reshape(q_rows * q_degree, w), quarter_senders, coarse_senders,
         *layers, after),
        (
            shaped(block, w), shaped(rows, block, dtype=half), shaped(q_degree, part, w), shaped(part, w),
            shaped(q_degree, part, w, dtype=short), shaped(c_degree, block, w, dtype=short),
            shaped(rows, w, dtype=short), shaped(*mats(2), dtype=half), shaped(*mats(4), dtype=half),
            shaped(*mats(3), dtype=half), shaped(*mats(4), dtype=half),
        ),
        [
            whole(block, w), whole(rows, block), whole(q_degree, part, w), whole(part, w), whole(q_degree, part, w),
            whole(c_degree, block, w), whole(rows, w), whole(*mats(2)), whole(*mats(4)), whole(*mats(3)),
            whole(*mats(4)),
        ],
        [], 16, 10**9,
    )
    edge_pieces = [own_edges, swapped(own_edges, "sub", 1)]
    mine = run(
        functools.partial(mean_kernel, lines), (1,), (), [whole(part + height, w)] * 2, (mine, theirs),
        shaped(part, w), whole(part, w), [], 6, 10**7,
    )
    other = swapped(mine, "sub", 1)

    quarter_nodes, to_next, to_previous = run(
        quarter_nodes_kernel, (1,), (flip,), [whole(part, w), whole(part, w), whole(2, q_margin)],
        (mine, other, quarter_halo), (shaped(q_rows, w), shaped(q_margin, w), shaped(q_margin, w)),
        [whole(q_rows, w), whole(q_margin, w), whole(q_margin, w)], [], 8, 10**8,
    )
    left = passed(to_next, "patch", 1)
    right = passed(to_previous, "patch", -1)
    bit = 2
    while bit < n_sub:
        edge_pieces += [swapped(value, "sub", bit) for value in edge_pieces]
        bit *= 2
    quarter_first = run(
        functools.partial(quarter_first_kernel, tile), (1,), (),
        [whole(q_degree, part, w), whole(q_rows, w), whole(part, w), whole(q_degree, part, w), whole(*mats(2))],
        (quarter_columns, quarter_nodes, mine, quarter_before, quarter_weights),
        shaped(q_degree, part, w), whole(q_degree, part, w),
        [pltpu.VMEM((q_rows, 2 * w), half), pltpu.VMEM((q_degree * tile, q_rows), half)], 16, 3 * 10**9,
    )
    quarter_mine, keep, both = run(
        quarter_second_kernel, (1,), (flip,),
        [
            whole(q_degree, part, w), whole(*quarter_pool_rows.shape), whole(part, w), whole(q_margin, w),
            whole(q_margin, w), whole(q_degree, part, w), whole(part, w), whole(*mats(2)), whole(*mats(4)),
        ],
        (quarter_columns, quarter_pool_rows, mine, left, right, quarter_first, quarter_sum, quarter_weights,
         quarter_later),
        (shaped(part, w), shaped(c_part, w), shaped(block, w)),
        [whole(part, w), whole(c_part, w), whole(block, w)],
        [pltpu.VMEM((2 * q_margin, 2 * w), half)], 16, 2 * 10**9,
    )

    theirs = swapped(both, "sub", 1)
    share = lax.dynamic_slice_in_dim(coarse_share, core * c_part, c_part, 0)
    own = (keep + theirs[:c_part]) * share
    share = lax.dynamic_slice_in_dim(coarse_share, (1 - core) * c_part, c_part, 0)
    own_partner = (both[:c_part] + theirs[c_part:]) * share
    quarter_other = swapped(quarter_mine, "sub", 1)
    pieces = [own] + [passed(own, "patch", -j) for j in range(1, n_patch)]
    partner = [own_partner] + [swapped(pieces[j], "sub", 1) for j in range(1, n_patch)]
    base, coarse_before, coarse_sum = run(
        functools.partial(base_kernel, n_sub), (1,), (sub_core,),
        [
            whole(rows, w), whole(part, w), whole(part, w), whole(rows, w), whole(*mats(3)),
            *[whole(*own_edges.shape)] * n_sub,
        ],
        (fine_columns, quarter_mine, quarter_other, hbm(fine_new), coarse_weights, *edge_pieces),
        (shaped(rows, w), shaped(c_degree, block, w), shaped(block, w)),
        [whole(rows, w), whole(c_degree, block, w), whole(block, w)],
        [pltpu.VMEM((q_rows, w), f32), pltpu.VMEM((block * c_degree, w), f32)], 16, 10**9,
    )
    return run(
        functools.partial(coarse_kernel, n_patch, c_tile), (1,), (patch_core,),
        [
            *[whole(c_part, w)] * (2 * n_patch), whole(c_degree, block, w), whole(c_degree, block, w),
            whole(block, w), whole(rows, block), whole(rows, w), whole(*mats(3)), whole(*mats(4)),
        ],
        (*pieces, *partner, coarse_columns, coarse_before, coarse_sum, chosen, base, coarse_weights, coarse_later),
        shaped(rows, w), in_hbm,
        [
            pltpu.VMEM((total, w), f32), pltpu.VMEM((total, 2 * w), half),
            pltpu.VMEM((c_degree * c_tile, total), half), pltpu.VMEM((c_degree, c_tile, w), f32),
            pltpu.VMEM((block, w), f32), pltpu.VMEM((rows, w), f32), pltpu.SemaphoreType.DMA((4,)),
        ],
        big, 2 * 10**9,
    )


def solution(mesh):
    split = P(("groups", "patch", "sub"))
    patches = P(("groups", "patch"))
    return jax.shard_map(
        on_device,
        mesh=mesh,
        in_specs=(
            split, split, split, split, split, patches, patches, patches, patches, split, P("groups"),
            P(), P(), P(), P(),
        ),
        out_specs=split,
        check_vma=False,
    )
```

time: 71.7 us -> 71.1 us (level)
  local copies, waits for them, and re-layouts: 0.06 us -> 8.65 us
  waiting for transfers between devices: 24.1 us -> 18 us
  Pallas kernels: 29.6 us -> 27.3 us
  starting transfers between devices: 17.2 us -> 16 us
    unnamed x24 -> x60, local copies, waits for them, and re-layouts: 0.06 us -> 8.65 us
    ppermute x10 -> x7, waiting for transfers between devices: 13.5 us -> 6.88 us  [passed(): lax.ppermute(value, axis, [(s, (s + steps) % count) for s in range(count)])]
    ppermute x10 -> x7, starting transfers between devices: 16 us -> 13.1 us  [passed(): lax.ppermute(value, axis, [(s, (s + steps) % count) for s in range(count)])]
    pallas_call x9 -> x10, Pallas kernels: 29.6 us -> 27.3 us  [run(): pl.pallas_call(kernel, out_shape=outs, grid_spec=pltpu.PrefetchScalarGrid...]
    ppermute x9 -> x11, starting transfers between devices: 1.22 us -> 2.88 us  [swapped(): return lax.ppermute(value, axis, [(s, s ^ bit) for s in range(count)])]
    ppermute x9 -> x11, waiting for transfers between devices: 10.6 us -> 11.1 us  [swapped(): return lax.ppermute(value, axis, [(s, s ^ bit) for s in range(count)])]
  transfers between devices with their start and end apart: 19 -> 18, of which waited for: 8 -> 7; matrix products, arithmetic and copies ran while one was open for 0% -> 0% of each run, Pallas kernels for 20% -> 26%
where the time goes in v1:
time: 71.1 us; the launch traced here: 70.7 us
  Pallas kernels  27.3 us (38%)
  waiting for transfers between devices  18 us (25%)
  starting transfers between devices  16 us (23%)
  local copies, waits for them, and re-layouts  8.65 us (12%)
    pallas_call x10, Pallas kernels, run(): pl.pallas_call(kernel, out_shape=outs, grid_spec=pltpu.PrefetchScalarGrid...  27.3 us
    ppermute x7, starting transfers between devices, passed(): lax.ppermute(value, axis, [(s, (s + steps) % count) for s in range(count)])  13.1 us
    ppermute x11, waiting for transfers between devices, swapped(): return lax.ppermute(value, axis, [(s, s ^ bit) for s in range(count)])  11.1 us
    unnamed x60, local copies, waits for them, and re-layouts  8.65 us
    ppermute x7, waiting for transfers between devices, passed(): lax.ppermute(value, axis, [(s, (s + steps) % count) for s in range(count)])  6.88 us
    ppermute x11, starting transfers between devices, swapped(): return lax.ppermute(value, axis, [(s, s ^ bit) for s in range(count)])  2.88 us
  transfers between devices with their start and end apart: 18, of which 7 were waited for; matrix products, arithmetic and copies ran while one was open for 0% of the time, Pallas kernels for 26%

profile of v1, /device:TPU:0, one launch (start us, length us, event | category | flops | bytes accessed | tf_op | source)
XLA Modules:
  0.0 70.7 jit_solution(12454315599222006577)
XLA Ops:
  0.0 1.5 %shard_map.145 = (f32[128,128]{1,0:T(8,128)S(1)}, f32[128,128]{1,0:T(8,128)S(1)}, f32[1024,128]{1,0:T(8,128)S(1)}, s32[6,1024]{1,0:T(8,128)S(1)}, s32[8,128]{1,0...) custom-call(s32[2,128]{1,0:T(2,128)} %lists.2, f32[1024,128]{1,0:T(8,128)} %nodes.1, s32[6,1024]{1,0:T(8,128)} %bitcast.16, ...), custom_call_target="tpu_custom_call" | custom-call | flops 100000000 | bytes 1000000 | tf_op jit(solution)/shard_map/pallas_call | solution.py:373
  2.1 5.0 %collective-permute-start.1 = (f32[128,128]{1,0:T(8,128)S(1)}, f32[128,128]{1,0:T(8,128)S(1)}, u32[]{:S(2)}, u32[]{:S(2)}) collective-permute-start(f32[128,128]{1,0:T(8,128)S(1)} %get-tuple-element.51), channel_id=1, source_target_pairs={{0,15},{1,0},{2,1},{3,2},{4,3},{5,4},{6,5},{7,6},{8,7},{9,8},{10,9... | collective-permute-start | bytes 196616 | tf_op jit(solution)/shard_map/ppermute | solution.py:387
  7.1 10.4 %shard_map.146 = (f32[1024,128]{1,0:T(8,128)S(1)}, f32[1024,128]{1,0:T(8,128)S(1)}, f32[1024,128]{1,0:T(8,128)S(1)}, f32[1024,128]{1,0:T(8,128)S(1)}, f32[1024,1...) custom-call(s32[1]{0:T(128)} %bitcast.1.flip, ...), custom_call_target="tpu_custom_call" | custom-call | flops 8000000000 | bytes 1000000 | tf_op jit(solution)/shard_map/pallas_call | solution.py:373
  18.8 1.0 %copy-done.21 = bf16[3,256,256]{2,1,0:T(8,128)(2,1)S(1)} copy-done((bf16[3,256,256]{2,1,0:T(8,128)(2,1)S(1)}, bf16[3,256,256]{2,1,0:T(8,128)(2,1)}, u32[]{:S(2)}) %copy-start.21) | copy-done | bytes 393240
  19.8 0.8 %copy-done.27 = f32[128,128]{1,0:T(8,128)S(1)} copy-done((f32[128,128]{1,0:T(8,128)S(1)}, f32[128,128]{1,0:T(8,128)}, u32[]{:S(2)}) %copy-start.27) | copy-done | bytes 65560
  21.5 3.7 %shard_map.147 = (f32[1024,128]{1,0:T(8,128)}, f32[520,128]{1,0:T(8,128)S(1)}, f32[520,128]{1,0:T(8,128)S(1)}) custom-call(s32[1]{0:T(128)} %bitcast.1.flip, s32[8,128]{1,0:T(8,128)S(1)} %get-tuple-element.48.pool.fine_pool, f32[1024,128]{1,0:T(8,128)S(1)} %get-tuple-element.49.nodes, f32[128,128]{1,0:T(8,128)S(1)} %copy-done.27, f32[128,128]{1,0:T(8,128)S(1)} %copy-done.29, ...), custom_call_target="tpu_custom_call" | custom-call | flops 4000000000 | bytes 1000000 | tf_op jit(solution)/shard_map/pallas_call | solution.py:373
  25.3 1.5 %collective-permute-done.2 = f32[520,128]{1,0:T(8,128)S(1)} collective-permute-done((f32[520,128]{1,0:T(8,128)S(1)}, f32[520,128]{1,0:T(8,128)S(1)}, u32[]{:S(2)}, u32[]{:S(2)}) %collective-permute-start.2) | collective-permute-done | bytes 266272 | tf_op jit(solution)/shard_map/ppermute | solution.py:392
  26.9 8.4 %collective-permute-done.3.theirs = f32[520,128]{1,0:T(8,128)S(1)} collective-permute-done((f32[520,128]{1,0:T(8,128)S(1)}, f32[520,128]{1,0:T(8,128)S(1)}, u32[]{:S(2)}, u32[]{:S(2)}) %collective-permute-start.3) | collective-permute-done | bytes 266272 | tf_op jit(solution)/shard_map/ppermute | solution.py:392
  36.2 1.0 %copy-done.3 = f32[3,256,128]{2,1,0:T(8,128)S(1)} copy-done((f32[3,256,128]{2,1,0:T(8,128)S(1)}, f32[3,256,128]{2,1,0:T(8,128)}, u32[]{:S(2)}) %copy-start.3) | copy-done | bytes 393240
  37.2 0.9 %copy-done.5 = f32[3,128,128]{2,1,0:T(8,128)S(1)} copy-done((f32[3,128,128]{2,1,0:T(8,128)S(1)}, f32[3,128,128]{2,1,0:T(8,128)}, u32[]{:S(2)}) %copy-start.5) | copy-done | bytes 196632
  38.1 0.9 %copy-done.7 = f32[3,128,128]{2,1,0:T(8,128)S(1)} copy-done((f32[3,128,128]{2,1,0:T(8,128)S(1)}, f32[3,128,128]{2,1,0:T(8,128)}, u32[]{:S(2)}) %copy-start.7) | copy-done | bytes 196632
  39.0 1.9 %shard_map.148 = (f32[256,128]{1,0:T(8,128)S(1)}, bf16[1024,256]{1,0:T(8,128)(2,1)S(1)}, f32[4,512,128]{2,1,0:T(8,128)S(1)}, f32[512,128]{1,0:T(8,128)S(1)}, s16...) custom-call(s32[2]{0:T(128)S(1)} %pad_add_fusion.flip.place, ...), custom_call_target="tpu_custom_call" | custom-call | flops 1000000000 | bytes 1000000 | tf_op jit(solution)/shard_map/pallas_call | solution.py:373
  43.3 3.6 %collective-permute-start.6 = (f32[128,128]{1,0:T(8,128)S(1)}, f32[128,128]{1,0:T(8,128)S(1)}, u32[]{:S(2)}, u32[]{:S(2)}) collective-permute-start(f32[128,128]{1,0:T(8,128)S(1)} %get-tuple-element.72), channel_id=1, source_target_pairs={{0,12},{4,0},{8,4},{12,8},{1,13},{5,1},{9,5},{13,9},{2,14},{6,2},{... | collective-permute-start | bytes 196616 | tf_op jit(solution)/shard_map/ppermute | solution.py:387
  47.0 1.5 %shard_map.151.before = f32[4,512,128]{2,1,0:T(8,128)S(1)} custom-call(s16[4,512,128]{2,1,0:T(8,128)(2,1)S(1)} %get-tuple-element.70.columns, f32[1024,128]{1,0:T(8,128)S(1)} %get-tuple-element.73.nodes, f32[512,128]{1,0:T(8,128)S(1)} %shard_map.149.mine, f32[4,512,128]{2,1,0:T(8,128)S(1)} %get-tuple-element.74.extra, ...), custom_call_target="tpu_custom_call" | custom-call | flops 3000000000 | bytes 1000000 | tf_op jit(solution)/shard_map/pallas_call | solution.py:373
  48.5 1.3 %collective-permute-done.5.left = f32[128,128]{1,0:T(8,128)S(1)} collective-permute-done((f32[128,128]{1,0:T(8,128)S(1)}, f32[128,128]{1,0:T(8,128)S(1)}, u32[]{:S(2)}, u32[]{:S(2)}) %collective-permute-start.5) | collective-permute-done | bytes 65568 | tf_op jit(solution)/shard_map/ppermute | solution.py:387
  49.7 1.7 %shard_map.152 = (f32[512,128]{1,0:T(8,128)S(1)}, f32[128,128]{1,0:T(8,128)S(1)}, f32[256,128]{1,0:T(8,128)S(1)}) custom-call(s32[1]{0:T(128)} %bitcast.1.flip, s16[4,512,128]{2,1,0:T(8,128)(2,1)S(1)} %get-tuple-element.70.columns, s32[8,128]{1,0:T(8,128)S(1)} %bitcast.15, f32[512,128]{1,0:T(8,128)S(1)} %shard_map.149.mine, ...), custom_call_target="tpu_custom_call" | custom-call | flops 2000000000 | bytes 1000000 | tf_op jit(solution)/shard_map/pallas_call | solution.py:373
  51.9 1.7 %collective-permute-start.17 = (f32[256,128]{1,0:T(8,128)}, f32[256,128]{1,0:T(8,128)S(1)}, u32[]{:S(2)}, u32[]{:S(2)}) collective-permute-start(f32[256,128]{1,0:T(8,128)} %collective-permute-done.15.refs_1_), channel_id=1, source_target_pairs={{0,2},{1,3},{2,0},{3,1},{4,6},{5,7},{6,4},{7,5},{8,10},{9,11},{10,... | collective-permute-start | bytes 393224 | tf_op jit(solution)/shard_map/ppermute | solution.py:392
  53.6 3.4 %collective-permute-start.8 = (f32[128,128]{1,0:T(8,128)S(1)}, f32[128,128]{1,0:T(8,128)S(1)}, u32[]{:S(2)}, u32[]{:S(2)}) collective-permute-start(f32[128,128]{1,0:T(8,128)S(1)} %get-tuple-element.92.refs_0_), channel_id=1, source_target_pairs={{0,12},{4,0},{8,4},{12,8},{1,13},{5,1},{9,5},{13,9},{2,14},{6,2},{... | collective-permute-start | bytes 196616 | tf_op jit(solution)/shard_map/ppermute | solution.py:387
  57.0 1.1 %collective-permute-done.16.refs_2_ = f32[256,128]{1,0:T(8,128)S(1)} collective-permute-done((f32[256,128]{1,0:T(8,128)}, f32[256,128]{1,0:T(8,128)S(1)}, u32[]{:S(2)}, u32[]{:S(2)}) %collective-permute-start.16) | collective-permute-done | bytes 131104 | tf_op jit(solution)/shard_map/ppermute | solution.py:392
  58.6 0.9 %collective-permute-done.8.refs_1_ = f32[128,128]{1,0:T(8,128)S(1)} collective-permute-done((f32[128,128]{1,0:T(8,128)S(1)}, f32[128,128]{1,0:T(8,128)S(1)}, u32[]{:S(2)}, u32[]{:S(2)}) %collective-permute-start.8) | collective-permute-done | bytes 65568 | tf_op jit(solution)/shard_map/ppermute | solution.py:387
  59.5 3.7 %collective-permute-done.9.refs_2_ = f32[128,128]{1,0:T(8,128)S(1)} collective-permute-done((f32[128,128]{1,0:T(8,128)S(1)}, f32[128,128]{1,0:T(8,128)S(1)}, u32[]{:S(2)}, u32[]{:S(2)}) %collective-permute-start.9) | collective-permute-done | bytes 65568 | tf_op jit(solution)/shard_map/ppermute | solution.py:387
  63.3 0.9 %collective-permute-done.10.refs_3_ = f32[128,128]{1,0:T(8,128)S(1)} collective-permute-done((f32[128,128]{1,0:T(8,128)S(1)}, f32[128,128]{1,0:T(8,128)S(1)}, u32[]{:S(2)}, u32[]{:S(2)}) %collective-permute-start.10) | collective-permute-done | bytes 65568 | tf_op jit(solution)/shard_map/ppermute | solution.py:387
  64.2 2.6 %shard_map.153 = (f32[1024,128]{1,0:T(8,128)S(1)}, f32[4,256,128]{2,1,0:T(8,128)S(1)}, f32[256,128]{1,0:T(8,128)S(1)}) custom-call(s32[2]{0:T(128)S(1)} %pad_add_fusion.1.place, s16[1024,128]{1,0:T(8,128)(2,1)S(1)} %copy-done.25, f32[512,128]{1,0:T(8,128)S(1)} %get-tuple-element.83.mine, f32[512,128]{1,0:T(8,128)S(1)} %collective-permute-done.14.other, ...), custom_call_target="tpu_custom_call" | custom-call | flops 1000000000 | bytes 1000000 | tf_op jit(solution)/shard_map/pallas_call | solution.py:373
  66.9 3.6 %shard_map.154 = f32[1024,128]{1,0:T(8,128)} custom-call(s32[2]{0:T(128)S(1)} %pad_add_fusion.flip.place, f32[128,128]{1,0:T(8,128)S(1)} %get-tuple-element.92.refs_0_, f32[128,128]{1,0:T(8,128)S(1)} %collective-permute-done.8.refs_1_, f32[128,128]{1,0:T(8,128)S(1)} %collective-permute-done.9.refs_2_, f32[128,128]{1,0:T(8,128)S(1)} %collective-permute-done.10.refs_3_, ...), custom_call_target="tpu_custom_call" | custom-call | flops 2000000000 | bytes 1000000 | tf_op jit(solution)/shard_map/pallas_call | solution.py:373
  (86 shorter events, 7.0 us)
Async XLA Ops:
  1.5 16.0 %copy-start.20 = (bf16[3,256,256]{2,1,0:T(8,128)(2,1)}, bf16[3,256,256]{2,1,0:T(8,128)(2,1)S(1)}, u32[]{:S(2)}) copy-start(bf16[3,256,256]{2,1,0:T(8,128)(2,1)S(1)} %get-tuple-element.53.weights.first_weights) | copy-start | bytes 1179652
  1.5 16.0 %collective-permute-start = (f32[128,128]{1,0:T(8,128)S(1)}, f32[128,128]{1,0:T(8,128)S(1)}, u32[]{:S(2)}, u32[]{:S(2)}) collective-permute-start(f32[128,128]{1,0:T(8,128)S(1)} %get-tuple-element.50), channel_id=1, source_target_pairs={{0,1},{1,2},{2,3},{3,4},{4,5},{5,6},{6,7},{7,8},{8,9},{9,10},{10,1... | collective-permute-start | bytes 196616 | tf_op jit(solution)/shard_map/ppermute | solution.py:387
  2.1 16.1 %collective-permute-start.1 = (f32[128,128]{1,0:T(8,128)S(1)}, f32[128,128]{1,0:T(8,128)S(1)}, u32[]{:S(2)}, u32[]{:S(2)}) collective-permute-start(f32[128,128]{1,0:T(8,128)S(1)} %get-tuple-element.51), channel_id=1, source_target_pairs={{0,15},{1,0},{2,1},{3,2},{4,3},{5,4},{6,5},{7,6},{8,7},{9,8},{10,9... | collective-permute-start | bytes 196616 | tf_op jit(solution)/shard_map/ppermute | solution.py:387
  21.5 14.7 %copy-start.12 = (s32[1024]{0:T(1024)S(1)}, s32[1024]{0:T(1024)}, u32[]{:S(2)}) copy-start(s32[1024]{0:T(1024)} %param.23) | copy-start | bytes 12292
  25.2 17.3 %copy-start.13 = (s32[2,128]{1,0:T(2,128)S(1)}, s32[2,128]{1,0:T(2,128)}, u32[]{:S(2)}) copy-start(s32[2,128]{1,0:T(2,128)} %lists.3) | copy-start | bytes 3076
  25.2 1.6 %collective-permute-start.2 = (f32[520,128]{1,0:T(8,128)S(1)}, f32[520,128]{1,0:T(8,128)S(1)}, u32[]{:S(2)}, u32[]{:S(2)}) collective-permute-start(f32[520,128]{1,0:T(8,128)S(1)} %get-tuple-element.69), channel_id=1, source_target_pairs={{0,1},{1,0},{2,3},{3,2},{4,5},{5,4},{6,7},{7,6},{8,9},{9,8},{10,11... | collective-permute-start | bytes 798728 | tf_op jit(solution)/shard_map/ppermute | solution.py:392
  26.8 8.5 %collective-permute-start.3 = (f32[520,128]{1,0:T(8,128)S(1)}, f32[520,128]{1,0:T(8,128)S(1)}, u32[]{:S(2)}, u32[]{:S(2)}) collective-permute-start(f32[520,128]{1,0:T(8,128)S(1)} %add.20._.mine), channel_id=1, source_target_pairs={{0,2},{1,3},{2,0},{3,1},{4,6},{5,7},{6,4},{7,5},{8,10},{9,11},{10,... | collective-permute-start | bytes 798728 | tf_op jit(solution)/shard_map/ppermute | solution.py:392
  35.5 7.0 %collective-permute-start.4 = (f32[512,128]{1,0:T(8,128)S(1)}, f32[512,128]{1,0:T(8,128)S(1)}, u32[]{:S(2)}, u32[]{:S(2)}) collective-permute-start(f32[512,128]{1,0:T(8,128)S(1)} %shard_map.149.mine), channel_id=1, source_target_pairs={{0,1},{1,0},{2,3},{3,2},{4,5},{5,4},{6,7},{7,6},{8,9},{9,8},{10,11... | collective-permute-start | bytes 786440 | tf_op jit(solution)/shard_map/ppermute | solution.py:392
  35.6 16.3 %collective-permute-start.15 = (f32[256,128]{1,0:T(8,128)}, f32[256,128]{1,0:T(8,128)}, u32[]{:S(2)}, u32[]{:S(2)}) collective-permute-start(f32[256,128]{1,0:T(8,128)} %bitcast.10.refs_0_), channel_id=1, source_target_pairs={{0,1},{1,0},{2,3},{3,2},{4,5},{5,4},{6,7},{7,6},{8,9},{9,8},{10,11... | collective-permute-start | bytes 393224 | tf_op jit(solution)/shard_map/ppermute | solution.py:392
  43.1 6.6 %collective-permute-start.5 = (f32[128,128]{1,0:T(8,128)S(1)}, f32[128,128]{1,0:T(8,128)S(1)}, u32[]{:S(2)}, u32[]{:S(2)}) collective-permute-start(f32[128,128]{1,0:T(8,128)S(1)} %get-tuple-element.71), channel_id=1, source_target_pairs={{0,4},{4,8},{8,12},{12,0},{1,5},{5,9},{9,13},{13,1},{2,6},{6,10},{... | collective-permute-start | bytes 196616 | tf_op jit(solution)/shard_map/ppermute | solution.py:387
  43.3 6.4 %collective-permute-start.6 = (f32[128,128]{1,0:T(8,128)S(1)}, f32[128,128]{1,0:T(8,128)S(1)}, u32[]{:S(2)}, u32[]{:S(2)}) collective-permute-start(f32[128,128]{1,0:T(8,128)S(1)} %get-tuple-element.72), channel_id=1, source_target_pairs={{0,12},{4,0},{8,4},{12,8},{1,13},{5,1},{9,5},{13,9},{2,14},{6,2},{... | collective-permute-start | bytes 196616 | tf_op jit(solution)/shard_map/ppermute | solution.py:387
  51.4 15.5 %copy-start.15 = (bf16[1024,256]{1,0:T(8,128)(2,1)S(1)}, bf16[1024,256]{1,0:T(8,128)(2,1)}, u32[]{:S(2)}) copy-start(bf16[1024,256]{1,0:T(8,128)(2,1)} %copy-done.14) | copy-start | bytes 1572868
  51.4 15.5 %copy-start.17 = (bf16[4,256,256]{2,1,0:T(8,128)(2,1)S(1)}, bf16[4,256,256]{2,1,0:T(8,128)(2,1)}, u32[]{:S(2)}) copy-start(bf16[4,256,256]{2,1,0:T(8,128)(2,1)} %copy-done.16) | copy-start | bytes 1572868
  51.4 15.5 %copy-start.23 = (s16[4,256,128]{2,1,0:T(8,128)(2,1)S(1)}, s16[4,256,128]{2,1,0:T(8,128)(2,1)}, u32[]{:S(2)}) copy-start(s16[4,256,128]{2,1,0:T(8,128)(2,1)} %copy-done.22) | copy-start | bytes 786436
  51.4 2.2 %collective-permute-start.7 = (f32[256,128]{1,0:T(8,128)S(1)}, f32[256,128]{1,0:T(8,128)S(1)}, u32[]{:S(2)}, u32[]{:S(2)}) collective-permute-start(f32[256,128]{1,0:T(8,128)S(1)} %get-tuple-element.79), channel_id=1, source_target_pairs={{0,1},{1,0},{2,3},{3,2},{4,5},{5,4},{6,7},{7,6},{8,9},{9,8},{10,11... | collective-permute-start | bytes 393224 | tf_op jit(solution)/shard_map/ppermute | solution.py:392
  51.5 6.6 %collective-permute-start.16 = (f32[256,128]{1,0:T(8,128)}, f32[256,128]{1,0:T(8,128)S(1)}, u32[]{:S(2)}, u32[]{:S(2)}) collective-permute-start(f32[256,128]{1,0:T(8,128)} %bitcast.10.refs_0_), channel_id=1, source_target_pairs={{0,2},{1,3},{2,0},{3,1},{4,6},{5,7},{6,4},{7,5},{8,10},{9,11},{10,... | collective-permute-start | bytes 393224 | tf_op jit(solution)/shard_map/ppermute | solution.py:392
  51.9 12.4 %collective-permute-start.17 = (f32[256,128]{1,0:T(8,128)}, f32[256,128]{1,0:T(8,128)S(1)}, u32[]{:S(2)}, u32[]{:S(2)}) collective-permute-start(f32[256,128]{1,0:T(8,128)} %collective-permute-done.15.refs_1_), channel_id=1, source_target_pairs={{0,2},{1,3},{2,0},{3,1},{4,6},{5,7},{6,4},{7,5},{8,10},{9,11},{10,... | collective-permute-start | bytes 393224 | tf_op jit(solution)/shard_map/ppermute | solution.py:392
  53.6 10.6 %collective-permute-start.14 = (f32[512,128]{1,0:T(8,128)S(1)}, f32[512,128]{1,0:T(8,128)S(1)}, u32[]{:S(2)}, u32[]{:S(2)}) collective-permute-start(f32[512,128]{1,0:T(8,128)S(1)} %get-tuple-element.83.mine), channel_id=1, source_target_pairs={{0,1},{1,0},{2,3},{3,2},{4,5},{5,4},{6,7},{7,6},{8,9},{9,8},{10,11... | collective-permute-start | bytes 786440 | tf_op jit(solution)/shard_map/ppermute | solution.py:392
  53.6 5.9 %collective-permute-start.8 = (f32[128,128]{1,0:T(8,128)S(1)}, f32[128,128]{1,0:T(8,128)S(1)}, u32[]{:S(2)}, u32[]{:S(2)}) collective-permute-start(f32[128,128]{1,0:T(8,128)S(1)} %get-tuple-element.92.refs_0_), channel_id=1, source_target_pairs={{0,12},{4,0},{8,4},{12,8},{1,13},{5,1},{9,5},{13,9},{2,14},{6,2},{... | collective-permute-start | bytes 196616 | tf_op jit(solution)/shard_map/ppermute | solution.py:387
  57.0 6.3 %collective-permute-start.9 = (f32[128,128]{1,0:T(8,128)S(1)}, f32[128,128]{1,0:T(8,128)S(1)}, u32[]{:S(2)}, u32[]{:S(2)}) collective-permute-start(f32[128,128]{1,0:T(8,128)S(1)} %get-tuple-element.92.refs_0_), channel_id=1, source_target_pairs={{0,8},{4,12},{8,0},{12,4},{1,9},{5,13},{9,1},{13,5},{2,10},{6,14},... | collective-permute-start | bytes 196616 | tf_op jit(solution)/shard_map/ppermute | solution.py:387
  58.1 6.1 %collective-permute-start.10 = (f32[128,128]{1,0:T(8,128)S(1)}, f32[128,128]{1,0:T(8,128)S(1)}, u32[]{:S(2)}, u32[]{:S(2)}) collective-permute-start(f32[128,128]{1,0:T(8,128)S(1)} %get-tuple-element.92.refs_0_), channel_id=1, source_target_pairs={{0,4},{4,8},{8,12},{12,0},{1,5},{5,9},{9,13},{13,1},{2,6},{6,10},{... | collective-permute-start | bytes 196616 | tf_op jit(solution)/shard_map/ppermute | solution.py:387
  59.5 7.3 %collective-permute-start.11 = (f32[128,128]{1,0:T(8,128)S(1)}, f32[128,128]{1,0:T(8,128)S(1)}, u32[]{:S(2)}, u32[]{:S(2)}) collective-permute-start(f32[128,128]{1,0:T(8,128)S(1)} %collective-permute-done.8.refs_1_), channel_id=1, source_target_pairs={{0,1},{1,0},{2,3},{3,2},{4,5},{5,4},{6,7},{7,6},{8,9},{9,8},{10,11... | collective-permute-start | bytes 196616 | tf_op jit(solution)/shard_map/ppermute | solution.py:392
  63.3 3.6 %collective-permute-start.12 = (f32[128,128]{1,0:T(8,128)S(1)}, f32[128,128]{1,0:T(8,128)S(1)}, u32[]{:S(2)}, u32[]{:S(2)}) collective-permute-start(f32[128,128]{1,0:T(8,128)S(1)} %collective-permute-done.9.refs_2_), channel_id=1, source_target_pairs={{0,1},{1,0},{2,3},{3,2},{4,5},{5,4},{6,7},{7,6},{8,9},{9,8},{10,11... | collective-permute-start | bytes 196616 | tf_op jit(solution)/shard_map/ppermute | solution.py:392
  64.2 2.6 %collective-permute-start.13 = (f32[128,128]{1,0:T(8,128)S(1)}, f32[128,128]{1,0:T(8,128)S(1)}, u32[]{:S(2)}, u32[]{:S(2)}) collective-permute-start(f32[128,128]{1,0:T(8,128)S(1)} %collective-permute-done.10.refs_3_), channel_id=1, source_target_pairs={{0,1},{1,0},{2,3},{3,2},{4,5},{5,4},{6,7},{7,6},{8,9},{9,8},{10,11... | collective-permute-start | bytes 196616 | tf_op jit(solution)/shard_map/ppermute | solution.py:392
  (24 other events, 153.5 us)
